TPU v7x, 512 devices: a whole 4x8x8 slice. The times are simulated.
512 devices in a mesh: panel: 8 (over x, core), sc: 64 (over z, y).
Axes of the slice: x: 4, y: 8, z: 8, core: 2. Of those that a mesh axis runs over, the one named last changes fastest.
Arguments:
- channel: bfloat16 [2, 2048, 1024, 128], P(None, 'sc', 'panel'), may hold values from -0.1875 to 0.1875
- received: bfloat16 [2, 2048, 1024], P(None, 'sc', 'panel'), may hold values from -6 to 6
- noise: float32 [2048], P('sc'), may hold values from 0.05 to 0.5
- steps: float32 [3, 2, 128, 128], replicated, may hold values from -0.5 to 0.5
- cotangent: float32 [2, 2048, 128], P(None, 'sc', 'panel'), may hold values from -6 to 6
- counts: int32 [64], P('sc'), may hold values from 1 to 32, 1280 in all
Outputs:
- grad_channel: bfloat16 [2, 2048, 1024, 128], P(None, 'sc', 'panel')
- grad_received: bfloat16 [2, 2048, 1024], P(None, 'sc', 'panel')
- grad_steps: float32 [3, 2, 128, 128], replicated
Inputs may be any that keep to these rules, and one draw needn't show every extreme that they name: `counts`: each block has between 1 and 32 rostered subcarriers, and some block has all 32.
All inputs are finite; a program needn't handle non-finite values.
Results may differ from a plain program's by a relative error of at most 0.014.
Values may be sent and summed in bfloat16 or wider, within the bound.
No kernel may reach another device: no remote copies, remote signals or barrier semaphores. Data moves between devices by JAX's collectives and lax.ppermute only.
A program may use at most 64 MiB of HBM per device.

v0:
```python
import jax
import jax.numpy as jnp
from jax import lax
from jax.sharding import PartitionSpec as P

EPS = 1e-06


def batched(matrix, vector):
    return jnp.einsum("suv,sv->su", matrix, vector, precision=lax.Precision.HIGHEST)


def shared(matrix, vector):
    return jnp.einsum("uv,sv->su", matrix, vector, precision=lax.Precision.HIGHEST)


def detector(gram_re, gram_im, match_re, match_im, steps, noise):
    sol_re = jnp.zeros_like(match_re)
    sol_im = jnp.zeros_like(match_im)
    resid_re, resid_im = (match_re, match_im)
    energy = jnp.sum(resid_re * resid_re + resid_im * resid_im, axis=1) + EPS
    earlier = energy
    prev_re, prev_im = (sol_re, sol_im)
    for index in range(steps.shape[0]):
        w_re, w_im = (steps[index, 0], steps[index, 1])
        dir_re = resid_re + shared(w_re, resid_re) - shared(w_im, resid_im)
        dir_im = resid_im + shared(w_re, resid_im) + shared(w_im, resid_re)
        if index > 0:
            ratio = (energy / earlier)[:, None]
            dir_re = dir_re + ratio * prev_re
            dir_im = dir_im + ratio * prev_im
        img_re = batched(gram_re, dir_re) - batched(gram_im, dir_im) + noise[:, None] * dir_re
        img_im = batched(gram_re, dir_im) + batched(gram_im, dir_re) + noise[:, None] * dir_im
        along = jnp.sum(dir_re * resid_re + dir_im * resid_im, axis=1)
        curvature = jnp.sum(dir_re * img_re + dir_im * img_im, axis=1) + EPS
        alpha = (along / curvature)[:, None]
        sol_re = sol_re + alpha * dir_re
        sol_im = sol_im + alpha * dir_im
        resid_re = resid_re - alpha * img_re
        resid_im = resid_im - alpha * img_im
        earlier = energy
        energy = jnp.sum(resid_re * resid_re + resid_im * resid_im, axis=1) + EPS
        prev_re, prev_im = (dir_re, dir_im)
    return (sol_re, sol_im)


def inner(form, left, right):
    return jnp.einsum(form, left, right, preferred_element_type=jnp.float32)


def partial_gram(chan, recv):
    h_re, h_im = (chan[0], chan[1])
    y_re, y_im = (recv[0], recv[1])
    gram_re = inner("sau,sav->suv", h_re, h_re) + inner("sau,sav->suv", h_im, h_im)
    gram_im = inner("sau,sav->suv", h_re, h_im) - inner("sau,sav->suv", h_im, h_re)
    match_re = inner("sau,sa->su", h_re, y_re) + inner("sau,sa->su", h_im, y_im)
    match_im = inner("sau,sa->su", h_re, y_im) - inner("sau,sa->su", h_im, y_re)
    return (gram_re, gram_im, match_re, match_im)


def adjoint(gram_re, gram_im, match_re, match_im, steps, noise_part, cot_re, cot_im):

    def forward(g_re, g_im, m_re, m_im, w_all):
        return detector(g_re, g_im, m_re, m_im, w_all, noise_part)

    outputs, pullback = jax.vjp(forward, gram_re, gram_im, match_re, match_im, steps)
    grads = pullback((cot_re, cot_im))
    sym = (grads[0] + jnp.swapaxes(grads[0], 1, 2)).astype(jnp.bfloat16)
    anti = (grads[1] - jnp.swapaxes(grads[1], 1, 2)).astype(jnp.bfloat16)
    return (sym, anti, grads[2].astype(jnp.bfloat16), grads[3].astype(jnp.bfloat16), grads[4])


def chain_rule(chan, recv, sym, anti, back_re, back_im):
    h_re, h_im = (chan[0], chan[1])
    yr32 = recv[0].astype(jnp.float32)
    yi32 = recv[1].astype(jnp.float32)
    br32 = back_re.astype(jnp.float32)
    bi32 = back_im.astype(jnp.float32)
    grad_hre = inner("sav,svu->sau", h_re, sym) - inner("sav,svu->sau", h_im, anti)
    grad_hre = grad_hre + yr32[:, :, None] * br32[:, None, :] + yi32[:, :, None] * bi32[:, None, :]
    grad_him = inner("sav,svu->sau", h_im, sym) + inner("sav,svu->sau", h_re, anti)
    grad_him = grad_him + yi32[:, :, None] * br32[:, None, :] - yr32[:, :, None] * bi32[:, None, :]
    grad_yre = inner("sau,su->sa", h_re, back_re) - inner("sau,su->sa", h_im, back_im)
    grad_yim = inner("sau,su->sa", h_im, back_re) + inner("sau,su->sa", h_re, back_im)
    grad_chan = jnp.stack([grad_hre, grad_him]).astype(jnp.bfloat16)
    grad_recv = jnp.stack([grad_yre, grad_yim]).astype(jnp.bfloat16)
    return (grad_chan, grad_recv)


def on_device(channel, received, noise, steps, cotangent, counts):
    panels = lax.axis_size("panel")
    width = channel.shape[1] // panels
    first = lax.axis_index("panel") * width
    cot_here = lax.all_to_all(cotangent, "panel", split_axis=1, concat_axis=2, tiled=True)
    position = first + jnp.arange(width, dtype=jnp.int32)
    live = (position < counts[0]).astype(jnp.float32)[:, None]
    cot_re = cot_here[0] * live
    cot_im = cot_here[1] * live
    noise_part = lax.dynamic_slice_in_dim(noise, first, width, 0)
    terms = partial_gram(channel, received)
    gram_re, gram_im, match_re, match_im = (
        lax.psum_scatter(
            terms[0].astype(jnp.bfloat16), "panel", scatter_dimension=0, tiled=True
        ).astype(jnp.float32),
        lax.psum_scatter(
            terms[1].astype(jnp.bfloat16), "panel", scatter_dimension=0, tiled=True
        ).astype(jnp.float32),
        lax.psum_scatter(
            terms[2].astype(jnp.bfloat16), "panel", scatter_dimension=0, tiled=True
        ).astype(jnp.float32),
        lax.psum_scatter(
            terms[3].astype(jnp.bfloat16), "panel", scatter_dimension=0, tiled=True
        ).astype(jnp.float32),
    )
    sym, anti, back_re, back_im, grad_w = adjoint(
        gram_re, gram_im, match_re, match_im, steps, noise_part, cot_re, cot_im
    )
    sym_all, anti_all, bre_all, bim_all = (
        lax.all_gather(sym, "panel", axis=0, tiled=True),
        lax.all_gather(anti, "panel", axis=0, tiled=True),
        lax.all_gather(back_re, "panel", axis=0, tiled=True),
        lax.all_gather(back_im, "panel", axis=0, tiled=True),
    )
    grad_channel, grad_received = chain_rule(channel, received, sym_all, anti_all, bre_all, bim_all)
    grad_steps = lax.psum(grad_w, ("panel", "sc"))
    return (grad_channel, grad_received, grad_steps)


def solution(mesh):
    return jax.shard_map(
        on_device,
        mesh=mesh,
        in_specs=(
            P(None, "sc", "panel", None),
            P(None, "sc", "panel"),
            P("sc"),
            P(),
            P(None, "sc", "panel"),
            P("sc"),
        ),
        out_specs=(P(None, "sc", "panel", None), P(None, "sc", "panel"), P()),
        check_vma=False,
    )
```

profile of v0, /device:TPU:1, one launch (start us, length us, event | category | flops | bytes accessed | tf_op | source)
XLA Modules:
  0.0 460.5 jit_solution(10206780318606603002)
XLA Ops:
  7.2 2.2 fusion.63
  9.4 1.5 add_convert_fusion
  11.1 0.7 reshape.159
  11.8 10.0 %all-to-all-start = ((f32[8,1,128]{2,1,0:T(1,128)}), f32[8,1,128]{2,1,0:T(1,128)S(1)}, u32[]{:S(2)}, u32[]{:S(2)}) async-start(f32[8,1,128]{2,1,0:T(1,128)} %reshape.159), calls=%async_computation.2 | async-start | bytes 8192 | tf_op jit(solution)/shard_map/all_to_all | solution.py:94
  21.8 0.5 fusion.47
  22.4 1.5 subtract_convert_fusion
  24.0 0.6 bitcast_convert_fusion
  24.6 0.4 fusion.50
  25.0 0.4 fusion.67
  25.4 0.4 fusion.65
  25.7 0.4 fusion.52
  26.8 1.3 dynamic-slice
  28.7 22.9 %all-reduce.8 = (bf16[32,128]{1,0:T(8,128)(2,1)S(1)}, bf16[32,128]{1,0:T(8,128)(2,1)S(1)}) all-reduce(bf16[32,128]{1,0:T(8,128)(2,1)S(1)} %add_convert_fusion.2, bf16[32,128]{1,0:T(8,128)(2,1)S(1)} %subtract_convert_fusion.2), channel_id=3, replica_groups=mesh['panel'=8,'sc'=64] {'panel'}, use_global_device_ids=true, to_apply=%region_1.0.clone | all-reduce | flops 8192 | bytes 32768
  52.5 0.5 broadcast.128
  53.0 0.7 reduce
  54.1 1.3 fusion.189
  55.3 1.2 fusion.191
  56.5 35.6 %reduce-scatter.5.cloned.1.call-done = bf16[4,128,128]{2,1,0:T(8,128)(2,1)} async-done(((bf16[32,128,128]{2,1,0:T(8,128)(2,1)}), bf16[4,128,128]{2,1,0:T(8,128)(2,1)}) %reduce-scatter.5.cloned.1.call-update) | async-done | bytes 131088 | tf_op jit(solution)/shard_map/reduce_scatter | solution.py:105
  92.2 1.3 fusion.190
  93.4 1.2 fusion.192
  96.0 1.2 fusion.194
  97.2 1.2 fusion.195
  98.4 1.2 fusion.193
  99.6 1.2 fusion.196
  102.2 1.2 fusion.200
  103.4 1.2 fusion.197
  104.6 1.2 fusion.199
  105.9 1.2 fusion.198
  107.1 0.3 multiply_reduce_fusion
  111.4 0.5 fusion.174
  112.6 0.6 fusion.178
  113.3 0.5 multiply_add_fusion
  114.3 1.9 fusion.69
  116.3 0.9 fusion.210
  117.2 0.9 fusion.209
  118.1 0.8 fusion.158
  118.9 0.8 convolution_add_fusion.14
  119.7 0.9 fusion.211
  120.6 0.9 fusion.212
  121.5 0.8 fusion.162
  122.3 0.8 fusion.37
  123.2 9.9 %all-gather.1 = bf16[8,4,128]{2,1,0:T(4,128)(2,1)S(1)} all-gather(bf16[1,4,128]{2,1,0:T(4,128)(2,1)S(1)} %fusion.37), channel_id=1, replica_groups=mesh['panel'=8,'sc'=64] {'panel'}, dimensions={0}, use_global_device_ids=true | all-gather | bytes 9216 | tf_op jit(solution)/shard_map/all_gather | solution.py:122
  133.1 0.8 fusion.24
  133.9 0.8 fusion.38
  134.7 10.0 %all-gather = bf16[8,4,128]{2,1,0:T(4,128)(2,1)S(1)} all-gather(bf16[1,4,128]{2,1,0:T(4,128)(2,1)S(1)} %fusion.38), channel_id=1, replica_groups=mesh['panel'=8,'sc'=64] {'panel'}, dimensions={0}, use_global_device_ids=true | all-gather | bytes 9216 | tf_op jit(solution)/shard_map/all_gather | solution.py:121
  144.7 0.9 fusion.218
  145.6 0.9 fusion.10
  146.5 0.6 fusion.39
  147.2 0.6 fusion.56
  147.9 0.7 fusion.54
  148.5 0.7 fusion.41
  149.3 0.6 pad_maximum_fusion.1
  151.4 0.3 fusion.7
  152.0 0.3 fusion.8
  152.6 0.3 fusion.9
  152.9 0.8 pad_add_fusion
  153.7 3.5 fusion.43
  157.2 2.2 fusion.59
  159.5 17.7 %all-gather.7.cloned.1.call-done = bf16[32,128,128]{2,1,0:T(8,128)(2,1)} async-done(((bf16[4,128,128]{2,1,0:T(8,128)(2,1)}), bf16[32,128,128]{2,1,0:T(8,128)(2,1)}) %all-gather.7.cloned.1.call-update) | async-done | bytes 1048592 | tf_op jit(solution)/shard_map/all_gather | solution.py:120
  177.2 3.3 fusion.5
  180.4 1.7 fusion.4
  182.4 2.7 copy.41
  185.1 267.1 %all-reduce.11.cloned.1.call-done = f32[3,2,128,128]{3,2,1,0:T(8,128)} async-done(((f32[3,2,128,128]{3,2,1,0:T(8,128)}), f32[3,2,128,128]{3,2,1,0:T(8,128)}) %all-reduce.11.cloned.1.call-update) | async-done | bytes 393232 | tf_op jit(solution)/shard_map/psum | solution.py:125
  452.2 1.8 copy.119
  (196 shorter events, 11.2 us)
Async XLA Ops:
  7.2 2.3 copy-start
  7.2 46.9 %reduce-scatter.3.cloned.1.call-start = ((), (), s32[]{:S(2)}) async-start(), calls=%async_computation.3 | async-start | bytes 1179648 | tf_op jit(solution)/shard_map/reduce_scatter | solution.py:102
  9.4 1.6 copy-start.48
  11.8 40.7 %all-to-all-start = ((f32[8,1,128]{2,1,0:T(1,128)}), f32[8,1,128]{2,1,0:T(1,128)S(1)}, u32[]{:S(2)}, u32[]{:S(2)}) async-start(f32[8,1,128]{2,1,0:T(1,128)} %reshape.159), calls=%async_computation.2 | async-start | bytes 8192 | tf_op jit(solution)/shard_map/all_to_all | solution.py:94
  21.8 70.3 %reduce-scatter.5.cloned.1.call-start = ((), (), s32[]{:S(2)}) async-start(), calls=%async_computation.4 | async-start | bytes 1179648 | tf_op jit(solution)/shard_map/reduce_scatter | solution.py:105
  22.4 1.6 copy-start.49
  23.9 129.8 %all-gather.5.cloned.1.call-start = ((), (), s32[]{:S(2)}) async-start(), calls=%async_computation.5 | async-start | bytes 1179648 | tf_op jit(solution)/shard_map/all_gather | solution.py:119
  25.0 26.7 %copy-start.4 = (f32[3,2,128,128]{3,2,1,0:T(8,128)S(1)}, f32[3,2,128,128]{3,2,1,0:T(8,128)}, u32[]{:S(2)}) copy-start(f32[3,2,128,128]{3,2,1,0:T(8,128)} %param.9) | copy-start | bytes 1179652
  25.4 27.1 %copy-start.53 = (f32[32]{0:T(128)S(1)}, f32[32]{0:T(128)}, u32[]{:S(2)}) copy-start(f32[32]{0:T(128)} %param.8) | copy-start | bytes 388
  51.6 49.9 %copy-start.23 = (bf16[4,128]{1,0:T(4,128)(2,1)}, bf16[4,128]{1,0:T(4,128)(2,1)S(1)}, u32[]{:S(2)}) copy-start(bf16[4,128]{1,0:T(4,128)(2,1)S(1)} %get-tuple-element.87) | copy-start | bytes 3076
  51.7 50.1 %copy-start.25 = (bf16[4,128]{1,0:T(4,128)(2,1)}, bf16[4,128]{1,0:T(4,128)(2,1)S(1)}, u32[]{:S(2)}) copy-start(bf16[4,128]{1,0:T(4,128)(2,1)S(1)} %get-tuple-element.86) | copy-start | bytes 3076
  52.4 58.7 %copy-start.45 = (f32[4]{0:T(128)}, f32[4]{0:T(128)S(1)}, u32[]{:S(2)}) copy-start(f32[4]{0:T(128)S(1)} %compare_convert_fusion) | copy-start | bytes 52
  52.5 58.5 %copy-start.38 = (f32[4]{0:T(128)}, f32[4]{0:T(128)S(1)}, u32[]{:S(2)}) copy-start(f32[4]{0:T(128)S(1)} %dynamic_slice.3) | copy-start | bytes 52
  53.9 58.3 %copy-start.36 = (f32[4,128]{1,0:T(4,128)}, f32[4,128]{1,0:T(4,128)S(1)}, u32[]{:S(2)}) copy-start(f32[4,128]{1,0:T(4,128)S(1)} %squeeze.55) | copy-start | bytes 6148
  54.0 58.5 %copy-start.37 = (f32[4,128]{1,0:T(4,128)}, f32[4,128]{1,0:T(4,128)S(1)}, u32[]{:S(2)}) copy-start(f32[4,128]{1,0:T(4,128)S(1)} %squeeze.53) | copy-start | bytes 6148
  54.0 53.4 %copy-start.1 = (bf16[4,128,128]{2,1,0:T(8,128)(2,1)S(1)}, bf16[4,128,128]{2,1,0:T(8,128)(2,1)}, u32[]{:S(2)}) copy-start(bf16[4,128,128]{2,1,0:T(8,128)(2,1)} %reduce-scatter.3.cloned.1.call-done) | copy-start | bytes 393220
  92.2 15.5 %copy-start.2 = (bf16[4,128,128]{2,1,0:T(8,128)(2,1)S(1)}, bf16[4,128,128]{2,1,0:T(8,128)(2,1)}, u32[]{:S(2)}) copy-start(bf16[4,128,128]{2,1,0:T(8,128)(2,1)} %reduce-scatter.5.cloned.1.call-done) | copy-start | bytes 393220
  94.9 18.9 %copy-start.43 = (f32[4,128]{1,0:T(4,128)}, f32[4,128]{1,0:T(4,128)S(1)}, u32[]{:S(2)}) copy-start(f32[4,128]{1,0:T(4,128)S(1)} %get-tuple-element.56) | copy-start | bytes 6148
  94.9 18.9 %copy-start.44 = (f32[4,128]{1,0:T(4,128)}, f32[4,128]{1,0:T(4,128)S(1)}, u32[]{:S(2)}) copy-start(f32[4,128]{1,0:T(4,128)S(1)} %get-tuple-element.57) | copy-start | bytes 6148
  94.9 18.9 %copy-start.51 = (f32[4]{0:T(128)}, f32[4]{0:T(128)S(1)}, u32[]{:S(2)}) copy-start(f32[4]{0:T(128)S(1)} %fusion.179) | copy-start | bytes 52
  95.1 18.7 %copy-start.9 = (f32[4,128]{1,0:T(4,128)}, f32[4,128]{1,0:T(4,128)S(1)}, u32[]{:S(2)}) copy-start(f32[4,128]{1,0:T(4,128)S(1)} %get-tuple-element.55) | copy-start | bytes 6148
  95.1 18.7 %copy-start.11 = (f32[4,128]{1,0:T(4,128)}, f32[4,128]{1,0:T(4,128)S(1)}, u32[]{:S(2)}) copy-start(f32[4,128]{1,0:T(4,128)S(1)} %get-tuple-element.54) | copy-start | bytes 6148
  95.5 6.7 %copy-start.50 = (f32[4]{0:T(128)}, f32[4]{0:T(128)S(1)}, u32[]{:S(2)}) copy-start(f32[4]{0:T(128)S(1)} %fusion.180) | copy-start | bytes 52
  101.3 12.5 %copy-start.15 = (f32[4,128]{1,0:T(4,128)}, f32[4,128]{1,0:T(4,128)S(1)}, u32[]{:S(2)}) copy-start(f32[4,128]{1,0:T(4,128)S(1)} %get-tuple-element.49) | copy-start | bytes 6148
  101.3 12.5 %copy-start.17 = (f32[4,128]{1,0:T(4,128)}, f32[4,128]{1,0:T(4,128)S(1)}, u32[]{:S(2)}) copy-start(f32[4,128]{1,0:T(4,128)S(1)} %get-tuple-element.50) | copy-start | bytes 6148
  101.9 11.9 %copy-start.7 = (f32[4,128]{1,0:T(4,128)}, f32[4,128]{1,0:T(4,128)S(1)}, u32[]{:S(2)}) copy-start(f32[4,128]{1,0:T(4,128)S(1)} %fusion.19) | copy-start | bytes 6148
  102.2 11.7 %copy-start.8 = (f32[4,128]{1,0:T(4,128)}, f32[4,128]{1,0:T(4,128)S(1)}, u32[]{:S(2)}) copy-start(f32[4,128]{1,0:T(4,128)S(1)} %fusion.17) | copy-start | bytes 6148
  107.5 6.4 %copy-start.33 = (f32[4,128]{1,0:T(4,128)}, f32[4,128]{1,0:T(4,128)S(1)}, u32[]{:S(2)}) copy-start(f32[4,128]{1,0:T(4,128)S(1)} %get-tuple-element.77) | copy-start | bytes 6148
  107.5 6.4 %copy-start.39 = (f32[4,128]{1,0:T(4,128)}, f32[4,128]{1,0:T(4,128)S(1)}, u32[]{:S(2)}) copy-start(f32[4,128]{1,0:T(4,128)S(1)} %get-tuple-element.76) | copy-start | bytes 6148
  108.1 5.8 %copy-start.19 = (f32[4,128]{1,0:T(4,128)}, f32[4,128]{1,0:T(4,128)S(1)}, u32[]{:S(2)}) copy-start(f32[4,128]{1,0:T(4,128)S(1)} %get-tuple-element.45) | copy-start | bytes 6148
  108.1 5.8 %copy-start.40 = (f32[4,128]{1,0:T(4,128)}, f32[4,128]{1,0:T(4,128)S(1)}, u32[]{:S(2)}) copy-start(f32[4,128]{1,0:T(4,128)S(1)} %get-tuple-element.68) | copy-start | bytes 6148
  108.8 2.3 copy-start.31
  109.8 4.1 copy-start.28
  109.8 4.1 copy-start.35
  109.8 4.1 copy-start.41
  110.4 2.7 copy-start.29
  111.3 2.7 copy-start.21
  112.2 1.7 copy-start.47
  112.6 1.4 copy-start.46
  113.2 0.8 copy-start.52
  113.3 0.7 copy-start.27
  113.3 0.7 copy-start.34
  113.3 0.7 copy-start.42
  116.2 60.9 %all-gather.7.cloned.1.call-start = ((), (), s32[]{:S(2)}) async-start(), calls=%async_computation.6 | async-start | bytes 1179648 | tf_op jit(solution)/shard_map/all_gather | solution.py:120
  146.5 3.4 copy-start.26
  146.5 3.7 copy-start.24
  147.1 3.3 copy-start.10
  147.1 3.3 copy-start.30
  147.1 3.6 copy-start.12
  147.2 3.6 copy-start.22
  147.2 4.5 copy-start.18
  147.2 4.5 copy-start.32
  147.2 4.8 %copy-start.16 = (f32[4,128]{1,0:T(4,128)S(1)}, f32[4,128]{1,0:T(4,128)}, u32[]{:S(2)}) copy-start(f32[4,128]{1,0:T(4,128)} %copy-done.15) | copy-start | bytes 6148
  147.2 4.8 %copy-start.20 = (f32[4,128]{1,0:T(4,128)S(1)}, f32[4,128]{1,0:T(4,128)}, u32[]{:S(2)}) copy-start(f32[4,128]{1,0:T(4,128)} %copy-done.19) | copy-start | bytes 6148
  149.2 303.0 %all-reduce.11.cloned.1.call-start = ((), (), s32[]{:S(2)}) async-start(), calls=%async_computation.7 | async-start | bytes 786432 | tf_op jit(solution)/shard_map/psum | solution.py:125
  153.7 3.5 copy-start.5
  157.2 19.9 %copy-start.13 = (f32[32,128]{1,0:T(8,128)S(1)}, f32[32,128]{1,0:T(8,128)}, u32[]{:S(2)}) copy-start(f32[32,128]{1,0:T(8,128)} %get-tuple-element.64) | copy-start | bytes 49156
  157.2 19.9 %copy-start.14 = (f32[32,128]{1,0:T(8,128)S(1)}, f32[32,128]{1,0:T(8,128)}, u32[]{:S(2)}) copy-start(f32[32,128]{1,0:T(8,128)} %get-tuple-element.67) | copy-start | bytes 49156
  177.2 3.3 copy-start.3
  177.2 3.3 copy-start.6
Sparse Core Ops, SparseCore 0:
  11.4 41.5 reduce-scatter.2
  55.8 36.3 reduce-scatter.4
  116.3 29.5 all-gather.4
  149.3 27.7 all-gather.6
  182.6 269.5 all-reduce.10
where the time goes:
time: 461 us; the launch traced here: 460 us
  waiting for transfers between devices  321 us (70%)
  matrix products  52.6 us (11%)
  blocking collectives  42.8 us (9%)
  between operations  16.1 us (3%)
  other arithmetic  10.3 us (2%)
  starting transfers between devices  10.2 us (2%)
  local copies, waits for them, and re-layouts  8.03 us (2%)
    psum x1, waiting for transfers between devices, on_device(): grad_steps = lax.psum(grad_w, ('panel', 'sc'))  267 us
    reduce_scatter x1, waiting for transfers between devices, on_device(): lax.psum_scatter(terms[1].astype(jnp.bfloat16), 'panel', scatter_dimensio...  35.6 us
    unnamed x1, blocking collectives  22.9 us
    dot_general x16, matrix products, inner(): return jnp.einsum(form, left, right, preferred_element_type=jnp.float32)  20.6 us
    dot_general x24, matrix products, batched(): jnp.einsum('suv,sv->su', matrix, vector, precision=lax.Precision.HIGHEST)  20 us
    all_gather x1, waiting for transfers between devices, on_device(): lax.all_gather(anti, 'panel', axis=0, tiled=True)  17.7 us
    dot_general x36, matrix products, shared(): jnp.einsum('uv,sv->su', matrix, vector, precision=lax.Precision.HIGHEST)  12 us
    all_to_all x1, starting transfers between devices, on_device(): lax.all_to_all(cotangent, 'panel', split_axis=1, concat_axis=2, tiled=True)  10 us
  transfers between devices with their start and end apart: 6, of which 3 were waited for; matrix products, arithmetic and copies ran while one was open for 9% of the time, Pallas kernels for 0%

commit v1 on v0

v1 whole, which is shorter than its diff:
```python
import functools

import jax
import jax.numpy as jnp
from jax import lax
from jax.experimental import pallas as pl
from jax.experimental.pallas import tpu as pltpu
from jax.sharding import PartitionSpec as P

EPS = 1e-06
F32 = jnp.float32
BF16 = jnp.bfloat16
NP = 8
SUB = 4
U = 128
A = 128
ROWS = 144
NN = (((1,), (0,)), ((), ()))
NT = (((1,), (1,)), ((), ()))
TN = (((0,), (0,)), ((), ()))


def dot(left, right, dims=NN):
    return lax.dot_general(left, right, dims, preferred_element_type=F32)


def split(value):
    high = value.astype(BF16)
    return high, (value - high.astype(F32)).astype(BF16)


def iota(shape, axis):
    return lax.broadcasted_iota(jnp.int32, shape, axis)


def rows_of(pieces, count):
    width = pieces[0][0].shape[1]
    at = iota((count, width), 0)
    out = jnp.zeros((count, width), F32)
    for k, (array, row) in enumerate(pieces):
        out = jnp.where(at == k, jnp.broadcast_to(array[row : row + 1], (count, width)), out)
    return out


def gram_kernel(chan_ref, recv_ref, cot_ref, out_ref, cot_rows):
    panel = lax.axis_index("panel")
    step = pl.program_id(0)

    @pl.when(step == 0)
    def _():
        place = (iota((16, U), 1) == panel * 16 + iota((16, U), 0)).astype(F32).astype(BF16)
        for part in range(2):
            high, low = split(cot_ref[part])
            cot_rows[2 * part] = dot(high, place, TN)
            cot_rows[2 * part + 1] = dot(low, place, TN)

    y_rows = jnp.concatenate([recv_ref[0], recv_ref[1]], axis=1)
    y_rows = jnp.concatenate([y_rows, jnp.zeros_like(y_rows)], axis=0)
    here = pl.ds(pl.multiple_of(step * 8, 8), 8)
    cots = [cot_rows[k, here, :] for k in range(4)]
    upper = iota((U, U), 0) <= iota((U, U), 1)
    for j in range(8):
        h_re, h_im = chan_ref[0, j], chan_ref[1, j]
        stack = jnp.concatenate([h_re, h_im], axis=0)
        other = jnp.concatenate([h_im, -h_re], axis=0)
        both = jnp.concatenate([stack, other], axis=1)
        left = jnp.concatenate([stack.T, y_rows], axis=0)
        prod = dot(left, both)
        packed = jnp.where(upper, prod[:U, :U], prod[:U, U:])
        match = prod[U + j : U + j + 1]
        m_re, m_im = match[:, :U], -match[:, U:]
        m_re_high, m_im_high = m_re.astype(BF16).astype(F32), m_im.astype(BF16).astype(F32)
        extra = rows_of(
            [(m_re_high, 0), (m_re - m_re_high, 0), (m_im_high, 0), (m_im - m_im_high, 0)]
            + [(c, j) for c in cots],
            16,
        )
        out_ref[j // SUB, j % SUB, 0:U, :] = packed.astype(BF16)
        out_ref[j // SUB, j % SUB, U:ROWS, :] = extra.astype(BF16)


def gram_call(channel, received, cot):
    return pl.pallas_call(
        gram_kernel,
        grid=(4,),
        out_shape=jax.ShapeDtypeStruct((NP, SUB, ROWS, U), BF16),
        in_specs=[
            pl.BlockSpec((2, 8, A, U), lambda i: (0, i, 0, 0)),
            pl.BlockSpec((2, 8, A), lambda i: (0, i, 0)),
            pl.BlockSpec((2, 16, 32), lambda i: (0, 0, 0)),
        ],
        out_specs=pl.BlockSpec((2, SUB, ROWS, U), lambda i: (i, 0, 0, 0)),
        scratch_shapes=[pltpu.VMEM((4, 32, U), F32)],
        name="gram",
    )(channel, received, cot)


def detect_kernel(noise_ref, count_ref, rx_ref, steps_ref, out_ref, gram_w, step_w):
    panel = lax.axis_index("panel")
    for k in range(3):
        w_re, w_im = steps_ref[k, 0], steps_ref[k, 1]
        re_hi, re_lo = split(w_re)
        im_hi, im_lo = split(w_im)
        for n, (re, im) in enumerate(((re_hi, im_hi), (re_lo, im_lo))):
            step_w[k, n, 0:U, 0:U] = re
            step_w[k, n, 0:U, U:] = -im
            step_w[k, n, U:, 0:U] = im
            step_w[k, n, U:, U:] = re
    row, col = iota((U, U), 0), iota((U, U), 1)
    at = iota((8, 2 * U), 0)
    at1 = iota((8, 1), 0)
    match = jnp.zeros((8, 2 * U), F32)
    cot = jnp.zeros((8, 2 * U), F32)
    for s in range(SUB):
        total = rx_ref[0, s].astype(F32)
        for p in range(1, NP):
            total = total + rx_ref[p, s].astype(F32)
        tri = total[0:U]
        flip = tri.T
        g_re = jnp.where(row <= col, tri, flip)
        g_im = jnp.where(row > col, tri, jnp.where(row < col, -flip, 0.0))
        re_hi, re_lo = split(g_re)
        im_hi, im_lo = split(g_im)
        for n, (re, im) in enumerate(((re_hi, im_hi), (re_lo, im_lo))):
            gram_w[s, n, 0:U, 0:U] = re
            gram_w[s, n, 0:U, U:] = -im
            gram_w[s, n, U:, 0:U] = im
            gram_w[s, n, U:, U:] = re
        ext = total[U:ROWS]
        m_row = jnp.concatenate([ext[0:1] + ext[1:2], ext[2:3] + ext[3:4]], axis=1)
        c_row = jnp.concatenate([ext[4:5] + ext[5:6], ext[6:7] + ext[7:8]], axis=1)
        alive = (panel * SUB + s < count_ref[0]).astype(F32)
        match = jnp.where(at == s, jnp.broadcast_to(m_row, (8, 2 * U)), match)
        cot = jnp.where(at == s, jnp.broadcast_to(c_row * alive, (8, 2 * U)), cot)
    sigma = jnp.zeros((8, 1), F32)
    for s in range(SUB):
        sigma = jnp.where(at1 == s, noise_ref[panel * SUB + s], sigma)

    def parts(v):
        high, low = split(v)
        return jnp.concatenate([high, low], axis=0)

    def times_gram(v):
        both = parts(v)
        out = sigma * v
        for s in range(SUB):
            one = dot(both, gram_w[s, 0])
            two = dot(both, gram_w[s, 1])
            out = out + jnp.where(at == s, one[0:8] + one[8:16] + two[0:8], 0.0)
        return out

    def times_step(k, v, dims):
        both = parts(v)
        one = dot(both, step_w[k, 0], dims)
        two = dot(both, step_w[k, 1], dims)
        return one[0:8] + one[8:16] + two[0:8]

    def total_of(a, b):
        return jnp.sum(a * b, axis=1, keepdims=True)

    r = match
    energy = total_of(r, r) + EPS
    rs, ds, qs, es, al, cs, bs = [], [], [], [energy], [], [], []
    for k in range(3):
        d = r + times_step(k, r, NT)
        ratio = None
        if k > 0:
            ratio = es[k] / es[k - 1]
            d = d + ratio * ds[-1]
        q = times_gram(d)
        along = total_of(d, r)
        curve = total_of(d, q) + EPS
        alpha = along / curve
        rs.append(r)
        ds.append(d)
        qs.append(q)
        al.append(alpha)
        cs.append(curve)
        bs.append(ratio)
        if k < 2:
            r = r - alpha * q
            es.append(total_of(r, r) + EPS)

    qb, db = [None] * 3, [None] * 3
    rb = None
    d_next = None
    e_bar = [jnp.zeros((8, 1), F32) for _ in range(3)]
    for k in (2, 1, 0):
        a_bar = total_of(cot, ds[k])
        if rb is not None:
            a_bar = a_bar - total_of(rb, qs[k])
        along_bar = a_bar / cs[k]
        curve_bar = -along_bar * al[k]
        d_bar = al[k] * cot + along_bar * rs[k] + curve_bar * qs[k]
        if d_next is not None:
            d_bar = d_bar + d_next
        if rb is None:
            qb[k] = curve_bar * ds[k]
            d_bar = d_bar + curve_bar * qs[k]
            rb = along_bar * ds[k]
        else:
            qb[k] = curve_bar * ds[k] - al[k] * rb
            d_bar = d_bar + times_gram(qb[k])
            rb = rb + along_bar * ds[k]
        db[k] = d_bar
        rb = rb + d_bar + times_step(k, d_bar, NN)
        if k > 0:
            b_bar = total_of(d_bar, ds[k - 1]) / es[k - 1]
            e_bar[k] = e_bar[k] + b_bar
            e_bar[k - 1] = e_bar[k - 1] - b_bar * bs[k]
            d_next = bs[k] * d_bar
        rb = rb + 2.0 * e_bar[k] * rs[k]

    for s in range(SUB):
        block = rows_of([(v, s) for v in (qb[0], ds[0], qb[1], ds[1], qb[2], ds[2], rb)], 8)
        both = jnp.concatenate([block[:, 0:U], block[:, U:]], axis=0).astype(BF16)
        for p in range(NP):
            out_ref[p, 16 * s : 16 * s + 16, :] = both
    zeros = jnp.zeros((8, 2 * U), F32)
    for k in range(3):
        d_hi, d_lo = split(db[k])
        r_hi, r_lo = split(rs[k])
        left = jnp.concatenate([d_hi, d_lo, d_hi, zeros.astype(BF16)], axis=0)
        right = jnp.concatenate([r_hi, r_hi, r_lo, zeros.astype(BF16)], axis=0)
        outer = dot(left, right, TN)
        g_re = (outer[0:U, 0:U] + outer[U:, U:]).astype(BF16)
        g_im = (outer[U:, 0:U] - outer[0:U, U:]).astype(BF16)
        for p in range(NP):
            base = 64 + k * 32
            out_ref[p, base : base + 16, :] = g_re[16 * p : 16 * p + 16]
            out_ref[p, base + 16 : base + 32, :] = g_im[16 * p : 16 * p + 16]


def detect_call(noise, counts, rx, steps):
    smem = pl.BlockSpec(memory_space=pltpu.SMEM)
    vmem = pl.BlockSpec(memory_space=pltpu.VMEM)
    return pl.pallas_call(
        detect_kernel,
        out_shape=jax.ShapeDtypeStruct((NP, 160, U), BF16),
        in_specs=[smem, smem, vmem, vmem],
        out_specs=vmem,
        scratch_shapes=[
            pltpu.VMEM((SUB, 2, 2 * U, 2 * U), BF16),
            pltpu.VMEM((3, 2, 2 * U, 2 * U), BF16),
        ],
        name="detect",
    )(noise, counts, rx, steps)


def chain_kernel(chan_ref, recv_ref, fac_ref, gchan_ref, grecv_ref):
    at = iota((8, U), 0)
    even = iota((16, U), 0) % 2 == 0
    gy_re = jnp.zeros((8, A), F32)
    gy_im = jnp.zeros((8, A), F32)
    y_re, y_im = recv_ref[0].astype(F32), recv_ref[1].astype(F32)
    for j in range(8):
        s = j % SUB
        fac = fac_ref[j // SUB, 16 * s : 16 * s + 16, :]
        chan = jnp.concatenate([chan_ref[0, j], chan_ref[1, j]], axis=0)
        prod = dot(fac, chan, NT)
        v_re = prod[0:8, 0:A] - prod[8:16, A:]
        v_im = prod[0:8, A:] + prod[8:16, 0:A]
        gy_re = jnp.where(at == j, jnp.broadcast_to(v_re[6:7], (8, A)), gy_re)
        gy_im = jnp.where(at == j, jnp.broadcast_to(v_im[6:7], (8, A)), gy_im)
        v_re = jnp.where(at == 7, jnp.broadcast_to(y_re[j : j + 1], (8, A)), v_re)
        v_im = jnp.where(at == 7, jnp.broadcast_to(y_im[j : j + 1], (8, A)), v_im)
        re_hi, re_lo = split(v_re)
        im_hi, im_lo = split(v_im)
        left = jnp.concatenate([re_hi, im_hi, re_lo, im_lo], axis=0)
        wide = fac.astype(F32)
        down = jnp.concatenate([wide[1:16], wide[0:1]], axis=0)
        up = jnp.concatenate([wide[15:16], wide[0:15]], axis=0)
        mate = jnp.where(even, down, up)
        g_re, g_im = mate[0:8], mate[8:16]
        right = jnp.concatenate(
            [jnp.concatenate([g_re, -g_im], axis=1), jnp.concatenate([g_im, g_re], axis=1)], axis=0
        ).astype(BF16)
        right = jnp.concatenate([right, right], axis=0)
        out = dot(left, right, TN)
        gchan_ref[0, j] = out[:, 0:U].astype(BF16)
        gchan_ref[1, j] = out[:, U:].astype(BF16)
    grecv_ref[0] = gy_re.astype(BF16)
    grecv_ref[1] = gy_im.astype(BF16)


def chain_call(channel, received, factors):
    return pl.pallas_call(
        chain_kernel,
        grid=(4,),
        out_shape=(
            jax.ShapeDtypeStruct((2, 32, A, U), BF16),
            jax.ShapeDtypeStruct((2, 32, A), BF16),
        ),
        in_specs=[
            pl.BlockSpec((2, 8, A, U), lambda i: (0, i, 0, 0)),
            pl.BlockSpec((2, 8, A), lambda i: (0, i, 0)),
            pl.BlockSpec((2, 64, U), lambda i: (i, 0, 0)),
        ],
        out_specs=(
            pl.BlockSpec((2, 8, A, U), lambda i: (0, i, 0, 0)),
            pl.BlockSpec((2, 8, A), lambda i: (0, i, 0)),
        ),
        name="chain",
    )(channel, received, factors)


def exchange(value, axis, groups=None):
    return lax.all_to_all(
        value, axis, split_axis=0, concat_axis=0, tiled=True, axis_index_groups=groups
    )


def on_device(channel, received, noise, steps, cotangent, counts):
    z_groups = [[8 * z + y for z in range(8)] for y in range(8)]
    y_groups = [[8 * z + y for y in range(8)] for z in range(8)]
    sent = gram_call(channel, received, jnp.swapaxes(cotangent, 1, 2))
    rx = exchange(sent, "panel")
    sent = detect_call(noise, counts, rx, steps)
    rx = exchange(sent, "panel")
    grad_channel, grad_received = chain_call(channel, received, rx)
    part = jnp.sum(rx[:, 64:].astype(F32), axis=0).astype(BF16)
    for groups in (y_groups, z_groups):
        every = exchange(jnp.broadcast_to(part, (8, 96, U)), "sc", groups)
        part = jnp.sum(every.astype(F32), axis=0).astype(BF16)
    every = exchange(jnp.broadcast_to(part, (8, 96, U)), "panel")
    grad_steps = every.astype(F32).reshape(8, 6, 16, U).transpose(1, 0, 2, 3)
    return (grad_channel, grad_received, grad_steps.reshape(3, 2, U, U))


def solution(mesh):
    return jax.shard_map(
        on_device,
        mesh=mesh,
        in_specs=(
            P(None, "sc", "panel", None),
            P(None, "sc", "panel"),
            P("sc"),
            P(),
            P(None, "sc", "panel"),
            P("sc"),
        ),
        out_specs=(P(None, "sc", "panel", None), P(None, "sc", "panel"), P()),
        check_vma=False,
    )
```

time: 461 us -> 97.6 us (0.21)
  waiting for transfers between devices: 321 us -> 15.8 us
  matrix products: 52.6 us -> 0 us
  Pallas kernels: 0 us -> 18.6 us
  between operations: 16.1 us -> 1.32 us
  other arithmetic: 10.3 us -> 0.12 us
  starting transfers between devices: 10.2 us -> 17.4 us
  local copies, waits for them, and re-layouts: 8.03 us -> 2.55 us
    psum x1 -> x0, waiting for transfers between devices: 267 us -> none  [on_device(): grad_steps = lax.psum(grad_w, ('panel', 'sc'))]
    dot_general x76 -> x0, matrix products: 52.6 us -> none  [the longest x16 20.6 us: inner(): return jnp.einsum(form, left, right, preferred_element_type=jnp.float32)]
    all_to_all x0 -> x3, blocking collectives: none -> 41.4 us  [exchange(): lax.all_to_all(value, axis, split_axis=0, concat_axis=0, tiled=True, axis...]
    reduce_scatter x2 -> x0, waiting for transfers between devices: 35.7 us -> none  [the longest x1 35.6 us: on_device(): lax.psum_scatter(terms[1].astype(jnp.bfloat16), 'panel', scatter_dimensio...]
    unnamed x1 -> x0, blocking collectives: 22.9 us -> none
    all_gather x2 -> x0, blocking collectives: 19.9 us -> none  [the longest x1 9.97 us: on_device(): lax.all_gather(back_re, 'panel', axis=0, tiled=True)]
    pallas_call x0 -> x3, Pallas kernels: none -> 18.6 us  [the longest x1 9.2 us: chain_call(): pl.pallas_call(chain_kernel, grid=(4,), out_shape=(jax.ShapeDtypeStruct((...]
    all_gather x2 -> x0, waiting for transfers between devices: 17.7 us -> none  [the longest x1 17.7 us: on_device(): lax.all_gather(anti, 'panel', axis=0, tiled=True)]
  transfers between devices with their start and end apart: 6 -> 2, of which waited for: 3 -> 1; matrix products, arithmetic and copies ran while one was open for 9% -> 0% of each run, Pallas kernels for 0% -> 9%
where the time goes in v1:
time: 97.6 us; the launch traced here: 97.1 us
  blocking collectives  41.4 us (42%)
  Pallas kernels  18.6 us (19%)
  starting transfers between devices  17.4 us (18%)
  waiting for transfers between devices  15.8 us (16%)
  local copies, waits for them, and re-layouts  2.55 us (3%)
  between operations  1.32 us (1%)
    all_to_all x3, blocking collectives, exchange(): lax.all_to_all(value, axis, split_axis=0, concat_axis=0, tiled=True, axis...  41.4 us
    all_to_all x2, starting transfers between devices, exchange(): lax.all_to_all(value, axis, split_axis=0, concat_axis=0, tiled=True, axis...  17.4 us
    all_to_all x2, waiting for transfers between devices, exchange(): lax.all_to_all(value, axis, split_axis=0, concat_axis=0, tiled=True, axis...  15.8 us
    pallas_call x1, Pallas kernels, chain_call(): pl.pallas_call(chain_kernel, grid=(4,), out_shape=(jax.ShapeDtypeStruct((...  9.2 us
    pallas_call x1, Pallas kernels, detect_call(): pl.pallas_call(detect_kernel, out_shape=jax.ShapeDtypeStruct((NP, 160, U)...  4.85 us
    pallas_call x1, Pallas kernels, gram_call(): pl.pallas_call(gram_kernel, grid=(4,), out_shape=jax.ShapeDtypeStruct((NP...  4.51 us
  transfers between devices with their start and end apart: 2, of which 1 were waited for; matrix products, arithmetic and copies ran while one was open for 0% of the time, Pallas kernels for 9%

profile of v1, /device:TPU:1, one launch (start us, length us, event | category | flops | bytes accessed | tf_op | source)
XLA Modules:
  0.0 97.1 jit_solution(13123769439423590749)
XLA Ops:
  0.6 4.5 %gram.1 = bf16[8,4,144,128]{3,2,1,0:T(8,128)(2,1)} custom-call(bf16[2,32,128,128]{3,2,1,0:T(8,128)(2,1)} %chan_ref.3, bf16[2,32,128]{2,1,0:T(8,128)(2,1)} %recv_ref.3, f32[2,16,32]{2,1,0:T(8,128)} %bitcast.8), custom_call_target="tpu_custom_call" | custom-call | tf_op jit(solution)/shard_map/gram/pallas_call | solution.py:83
  5.1 10.3 %all-to-all-start = ((bf16[8,4,144,128]{3,2,1,0:T(8,128)(2,1)}), bf16[8,4,144,128]{3,2,1,0:T(8,128)(2,1)S(1)}, u32[]{:S(2)}, u32[]{:S(2)}) async-start(bf16[8,4,144,128]{3,2,1,0:T(8,128)(2,1)} %gram.1), calls=%async_computation | async-start | bytes 2359296 | tf_op jit(solution)/shard_map/all_to_all | solution.py:308
  16.1 15.8 %all-to-all-done.rx_ref = bf16[8,4,144,128]{3,2,1,0:T(8,128)(2,1)S(1)} async-done(((bf16[8,4,144,128]{3,2,1,0:T(8,128)(2,1)}), bf16[8,4,144,128]{3,2,1,0:T(8,128)(2,1)S(1)}, u32[]{:S(2)}, u32[]{:S(2)}) %all-to-all-start) | async-done | bytes 1179680 | tf_op jit(solution)/shard_map/all_to_all | solution.py:308
  31.8 0.0 copy-start
  31.8 1.0 %copy-done = bf16[8,4,144,128]{3,2,1,0:T(8,128)(2,1)} copy-done((bf16[8,4,144,128]{3,2,1,0:T(8,128)(2,1)}, bf16[8,4,144,128]{3,2,1,0:T(8,128)(2,1)S(1)}, u32[]{:S(2)}) %copy-start) | copy-done | bytes 1179672
  32.9 4.8 %detect.1 = bf16[8,160,128]{2,1,0:T(8,128)(2,1)} custom-call(f32[32]{0:T(128)} %noise_ref.1, s32[1]{0:T(128)S(6)} %copy.11.count_ref, bf16[8,4,144,128]{3,2,1,0:T(8,128)(2,1)} %copy-done, f32[3,2,128,128]{3,2,1,0:T(8,128)} %steps_ref.1), custom_call_target="tpu_custom_call" | custom-call | tf_op jit(solution)/shard_map/detect/pallas_call | solution.py:237
  37.7 11.8 %all_to_all.25.fac_ref = bf16[8,160,128]{2,1,0:T(8,128)(2,1)S(1)} all-to-all(bf16[8,160,128]{2,1,0:T(8,128)(2,1)} %detect.1), channel_id=1, replica_groups=mesh['panel'=8,'sc'=64] {'panel'}, dimensions={0} | all-to-all | bytes 655360 | tf_op jit(solution)/shard_map/all_to_all | solution.py:308
  49.5 0.0 copy-start.1
  49.5 11.7 %all_to_all.26 = bf16[8,96,128]{2,1,0:T(8,128)(2,1)S(1)} all-to-all(bf16[8,96,128]{2,1,0:T(8,128)(2,1)S(1)} %broadcast_in_dim.9), channel_id=1, replica_groups={{0,1,2,3,4,5,6,7},{8,9,10,11,12,13,14,15},{16,17,18,19,20,21,22,23},{24..., dimensions={0} | all-to-all | bytes 393216 | tf_op jit(solution)/shard_map/all_to_all | solution.py:308
  61.4 17.9 %all_to_all.27 = bf16[8,96,128]{2,1,0:T(8,128)(2,1)S(1)} all-to-all(bf16[8,96,128]{2,1,0:T(8,128)(2,1)S(1)} %broadcast_in_dim.10), channel_id=1, replica_groups={{0,8,16,24,32,40,48,56},{1,9,17,25,33,41,49,57},{2,10,18,26,34,42,50,58..., dimensions={0} | all-to-all | bytes 393216 | tf_op jit(solution)/shard_map/all_to_all | solution.py:308
  79.3 0.7 broadcast_in_dim.11
  80.0 7.1 %all-to-all-start.4 = ((bf16[8,96,128]{2,1,0:T(8,128)(2,1)}), bf16[8,96,128]{2,1,0:T(8,128)(2,1)S(1)}, u32[]{:S(2)}, u32[]{:S(2)}) async-start(bf16[8,96,128]{2,1,0:T(8,128)(2,1)} %broadcast_in_dim.11), calls=%async_computation.4 | async-start | bytes 393216 | tf_op jit(solution)/shard_map/all_to_all | solution.py:308
  87.0 0.0 copy-done.1
  87.0 9.2 %chain.1 = (bf16[2,32,128,128]{3,2,1,0:T(8,128)(2,1)}, bf16[2,32,128]{2,1,0:T(8,128)(2,1)}) custom-call(bf16[2,32,128,128]{3,2,1,0:T(8,128)(2,1)} %chan_ref.3, bf16[2,32,128]{2,1,0:T(8,128)(2,1)} %recv_ref.3, bf16[8,160,128]{2,1,0:T(8,128)(2,1)} %copy-done.1), custom_call_target="tpu_custom_call" | custom-call | tf_op jit(solution)/shard_map/chain/pallas_call | solution.py:287
  96.2 0.0 all-to-all-done.4
  96.3 0.8 copy.10
  (6 shorter events, 0.2 us)
Async XLA Ops:
  5.1 26.7 %all-to-all-start = ((bf16[8,4,144,128]{3,2,1,0:T(8,128)(2,1)}), bf16[8,4,144,128]{3,2,1,0:T(8,128)(2,1)S(1)}, u32[]{:S(2)}, u32[]{:S(2)}) async-start(bf16[8,4,144,128]{3,2,1,0:T(8,128)(2,1)} %gram.1), calls=%async_computation | async-start | bytes 2359296 | tf_op jit(solution)/shard_map/all_to_all | solution.py:308
  31.8 1.0 %copy-start = (bf16[8,4,144,128]{3,2,1,0:T(8,128)(2,1)}, bf16[8,4,144,128]{3,2,1,0:T(8,128)(2,1)S(1)}, u32[]{:S(2)}) copy-start(bf16[8,4,144,128]{3,2,1,0:T(8,128)(2,1)S(1)} %all-to-all-done.rx_ref) | copy-start | bytes 3538948
  49.5 37.6 %copy-start.1 = (bf16[8,160,128]{2,1,0:T(8,128)(2,1)}, bf16[8,160,128]{2,1,0:T(8,128)(2,1)S(1)}, u32[]{:S(2)}) copy-start(bf16[8,160,128]{2,1,0:T(8,128)(2,1)S(1)} %all_to_all.25.fac_ref) | copy-start | bytes 983044
  80.0 16.3 %all-to-all-start.4 = ((bf16[8,96,128]{2,1,0:T(8,128)(2,1)}), bf16[8,96,128]{2,1,0:T(8,128)(2,1)S(1)}, u32[]{:S(2)}, u32[]{:S(2)}) async-start(bf16[8,96,128]{2,1,0:T(8,128)(2,1)} %broadcast_in_dim.11), calls=%async_computation.4 | async-start | bytes 393216 | tf_op jit(solution)/shard_map/all_to_all | solution.py:308

commit v2 on v1

--- a/solution.py
+++ b/solution.py
@@ -42,9 +42,10 @@
     return out
 
 
-def gram_kernel(chan_ref, recv_ref, cot_ref, out_ref, cot_rows):
+def gram_kernel(own, chan_ref, recv_ref, cot_ref, out_ref, cot_rows):
     panel = lax.axis_index("panel")
     step = pl.program_id(0)
+    core = lax.rem(panel + (0 if own else 1), 2)
 
     @pl.when(step == 0)
     def _():
@@ -56,42 +57,44 @@
 
     y_rows = jnp.concatenate([recv_ref[0], recv_ref[1]], axis=1)
     y_rows = jnp.concatenate([y_rows, jnp.zeros_like(y_rows)], axis=0)
-    here = pl.ds(pl.multiple_of(step * 8, 8), 8)
-    cots = [cot_rows[k, here, :] for k in range(4)]
     upper = iota((U, U), 0) <= iota((U, U), 1)
-    for j in range(8):
-        h_re, h_im = chan_ref[0, j], chan_ref[1, j]
+    at = iota((8, 2 * U), 0)
+    for j in range(SUB):
+        row = core * SUB + j
+        h_re, h_im = chan_ref[0, row], chan_ref[1, row]
         stack = jnp.concatenate([h_re, h_im], axis=0)
         other = jnp.concatenate([h_im, -h_re], axis=0)
         both = jnp.concatenate([stack, other], axis=1)
         left = jnp.concatenate([stack.T, y_rows], axis=0)
         prod = dot(left, both)
         packed = jnp.where(upper, prod[:U, :U], prod[:U, U:])
-        match = prod[U + j : U + j + 1]
+        match = jnp.sum(jnp.where(at == row, prod[U : U + 8], 0.0), axis=0, keepdims=True)
         m_re, m_im = match[:, :U], -match[:, U:]
         m_re_high, m_im_high = m_re.astype(BF16).astype(F32), m_im.astype(BF16).astype(F32)
         extra = rows_of(
             [(m_re_high, 0), (m_re - m_re_high, 0), (m_im_high, 0), (m_im - m_im_high, 0)]
-            + [(c, j) for c in cots],
+            + [(cot_rows[k, pl.ds(step * 8 + row, 1), :], 0) for k in range(4)],
             16,
         )
-        out_ref[j // SUB, j % SUB, 0:U, :] = packed.astype(BF16)
-        out_ref[j // SUB, j % SUB, U:ROWS, :] = extra.astype(BF16)
-
-
-def gram_call(channel, received, cot):
+        out_ref[0, j, 0:U, :] = packed.astype(BF16)
+        out_ref[0, j, U:ROWS, :] = extra.astype(BF16)
+
+
+def gram_call(own, channel, received, cot):
     return pl.pallas_call(
-        gram_kernel,
+        functools.partial(gram_kernel, own),
         grid=(4,),
-        out_shape=jax.ShapeDtypeStruct((NP, SUB, ROWS, U), BF16),
+        out_shape=jax.ShapeDtypeStruct((NP // 2, SUB, ROWS, U), BF16),
         in_specs=[
             pl.BlockSpec((2, 8, A, U), lambda i: (0, i, 0, 0)),
             pl.BlockSpec((2, 8, A), lambda i: (0, i, 0)),
             pl.BlockSpec((2, 16, 32), lambda i: (0, 0, 0)),
         ],
-        out_specs=pl.BlockSpec((2, SUB, ROWS, U), lambda i: (i, 0, 0, 0)),
+        out_specs=pl.BlockSpec((1, SUB, ROWS, U), lambda i: (i, 0, 0, 0)),
         scratch_shapes=[pltpu.VMEM((4, 32, U), F32)],
-        name="gram",
+        compiler_params=pltpu.CompilerParams(vmem_limit_bytes=8 << 20),
+        cost_estimate=pl.CostEstimate(flops=3 * 10**8, bytes_accessed=3 << 20, transcendentals=0),
+        name="gram_own" if own else "gram_mate",
     )(channel, received, cot)
 
 
@@ -113,7 +116,7 @@
     cot = jnp.zeros((8, 2 * U), F32)
     for s in range(SUB):
         total = rx_ref[0, s].astype(F32)
-        for p in range(1, NP):
+        for p in range(1, NP // 2):
             total = total + rx_ref[p, s].astype(F32)
         tri = total[0:U]
         flip = tri.T
@@ -243,6 +246,8 @@
             pltpu.VMEM((SUB, 2, 2 * U, 2 * U), BF16),
             pltpu.VMEM((3, 2, 2 * U, 2 * U), BF16),
         ],
+        compiler_params=pltpu.CompilerParams(vmem_limit_bytes=16 << 20),
+        cost_estimate=pl.CostEstimate(flops=10**9, bytes_accessed=4 << 20, transcendentals=0),
         name="detect",
     )(noise, counts, rx, steps)
 
@@ -300,8 +305,29 @@
             pl.BlockSpec((2, 8, A, U), lambda i: (0, i, 0, 0)),
             pl.BlockSpec((2, 8, A), lambda i: (0, i, 0)),
         ),
+        compiler_params=pltpu.CompilerParams(vmem_limit_bytes=8 << 20),
+        cost_estimate=pl.CostEstimate(flops=10**9, bytes_accessed=20 << 20, transcendentals=0),
         name="chain",
     )(channel, received, factors)
+
+
+def widen_kernel(in_ref, out_ref):
+    for p in range(NP):
+        for k in range(6):
+            rows = in_ref[p, 16 * k : 16 * k + 16, :].astype(F32)
+            out_ref[k // 2, k % 2, 16 * p : 16 * p + 16, :] = rows
+
+
+def widen_call(every):
+    vmem = pl.BlockSpec(memory_space=pltpu.VMEM)
+    return pl.pallas_call(
+        widen_kernel,
+        out_shape=jax.ShapeDtypeStruct((3, 2, U, U), F32),
+        in_specs=[vmem],
+        out_specs=vmem,
+        compiler_params=pltpu.CompilerParams(vmem_limit_bytes=4 << 20),
+        name="widen",
+    )(every)
 
 
 def exchange(value, axis, groups=None):
@@ -313,18 +339,21 @@
 def on_device(channel, received, noise, steps, cotangent, counts):
     z_groups = [[8 * z + y for z in range(8)] for y in range(8)]
     y_groups = [[8 * z + y for y in range(8)] for z in range(8)]
-    sent = gram_call(channel, received, jnp.swapaxes(cotangent, 1, 2))
-    rx = exchange(sent, "panel")
-    sent = detect_call(noise, counts, rx, steps)
-    rx = exchange(sent, "panel")
-    grad_channel, grad_received = chain_call(channel, received, rx)
-    part = jnp.sum(rx[:, 64:].astype(F32), axis=0).astype(BF16)
+    cot = jnp.swapaxes(cotangent, 1, 2)
+    away = gram_call(False, channel, received, cot)
+    got = lax.ppermute(away, "panel", [(p, p ^ 1) for p in range(NP)])
+    own = gram_call(True, channel, received, cot)
+    pair = (own.astype(F32) + got.astype(F32)).astype(BF16)
+    rx = exchange(pair, "panel", [[0, 2, 4, 6], [1, 3, 5, 7]])
+    both = exchange(detect_call(noise, counts, rx, steps), "panel")
+    part = jnp.sum(both[:, 64:].astype(F32), axis=0).astype(BF16)
+    grad_channel, grad_received = chain_call(channel, received, both)
     for groups in (y_groups, z_groups):
         every = exchange(jnp.broadcast_to(part, (8, 96, U)), "sc", groups)
         part = jnp.sum(every.astype(F32), axis=0).astype(BF16)
+    part, grad_received = lax.optimization_barrier((part, grad_received))
     every = exchange(jnp.broadcast_to(part, (8, 96, U)), "panel")
-    grad_steps = every.astype(F32).reshape(8, 6, 16, U).transpose(1, 0, 2, 3)
-    return (grad_channel, grad_received, grad_steps.reshape(3, 2, U, U))
+    return (grad_channel, grad_received, widen_call(every))
 
 
 def solution(mesh):

time: 97.6 us -> 88.3 us (0.905)
  blocking collectives: 41.4 us -> 34.9 us
  waiting for transfers between devices: 15.8 us -> 9.7 us
  starting transfers between devices: 17.4 us -> 21.3 us
  Pallas kernels: 18.6 us -> 15.5 us
  local copies, waits for them, and re-layouts: 2.55 us -> 3.8 us
    ppermute x0 -> x1, starting transfers between devices: none -> 8.75 us  [on_device(): got = lax.ppermute(away, 'panel', [(p, p ^ 1) for p in range(NP)])]
    all_to_all x3, blocking collectives: 41.4 us -> 34.9 us  [exchange(): lax.all_to_all(value, axis, split_axis=0, concat_axis=0, tiled=True, axis...]
    all_to_all x2, waiting for transfers between devices: 15.8 us -> 9.7 us  [exchange(): lax.all_to_all(value, axis, split_axis=0, concat_axis=0, tiled=True, axis...]
    all_to_all x2, starting transfers between devices: 17.4 us -> 12.6 us  [exchange(): lax.all_to_all(value, axis, split_axis=0, concat_axis=0, tiled=True, axis...]
    unnamed x4 -> x14, local copies, waits for them, and re-layouts: 1.02 us -> 3.05 us
    pallas_call x1, Pallas kernels: 4.85 us -> 3.23 us  [detect_call(): pl.pallas_call(detect_kernel, out_shape=jax.ShapeDtypeStruct((NP, 160, U)...]
    pallas_call x1 -> x3, Pallas kernels: 4.51 us -> 4.02 us  [the longest x2 3.25 us: gram_call(): pl.pallas_call(functools.partial(gram_kernel, own), grid=(4,), out_shape=...]
  transfers between devices with their start and end apart: 2 -> 3, of which waited for: 1 -> 2; matrix products, arithmetic and copies ran while one was open for 0% -> 0% of each run, Pallas kernels for 9% -> 11%
where the time goes in v2:
time: 88.3 us; the launch traced here: 87.8 us
  blocking collectives  34.9 us (40%)
  starting transfers between devices  21.3 us (24%)
  Pallas kernels  15.5 us (18%)
  waiting for transfers between devices  9.7 us (11%)
  local copies, waits for them, and re-layouts  3.8 us (4%)
  between operations  1.41 us (2%)
  other arithmetic  1.06 us (1%)
    all_to_all x3, blocking collectives, exchange(): lax.all_to_all(value, axis, split_axis=0, concat_axis=0, tiled=True, axis...  34.9 us
    all_to_all x2, starting transfers between devices, exchange(): lax.all_to_all(value, axis, split_axis=0, concat_axis=0, tiled=True, axis...  12.6 us
    all_to_all x2, waiting for transfers between devices, exchange(): lax.all_to_all(value, axis, split_axis=0, concat_axis=0, tiled=True, axis...  9.7 us
    ppermute x1, starting transfers between devices, on_device(): got = lax.ppermute(away, 'panel', [(p, p ^ 1) for p in range(NP)])  8.75 us
    pallas_call x1, Pallas kernels, chain_call(): pl.pallas_call(chain_kernel, grid=(4,), out_shape=(jax.ShapeDtypeStruct((...  8.3 us
    pallas_call x2, Pallas kernels, gram_call(): pl.pallas_call(functools.partial(gram_kernel, own), grid=(4,), out_shape=...  3.25 us
    pallas_call x1, Pallas kernels, detect_call(): pl.pallas_call(detect_kernel, out_shape=jax.ShapeDtypeStruct((NP, 160, U)...  3.23 us
    unnamed x14, local copies, waits for them, and re-layouts  3.05 us
  transfers between devices with their start and end apart: 3, of which 2 were waited for; matrix products, arithmetic and copies ran while one was open for 0% of the time, Pallas kernels for 11%

profile of v2, /device:TPU:1, one launch (start us, length us, event | category | flops | bytes accessed | tf_op | source)
XLA Modules:
  0.0 87.8 jit_solution(3589939368981460854)
XLA Ops:
  0.6 0.0 copy-start
  0.6 1.6 %copy-done = bf16[2,32,128,128]{3,2,1,0:T(8,128)(2,1)S(1)} copy-done((bf16[2,32,128,128]{3,2,1,0:T(8,128)(2,1)S(1)}, bf16[2,32,128,128]{3,2,1,0:T(8,128)(2,1)}, u32[]{:S(2)}) %copy-start) | copy-done | bytes 2097176
  2.2 0.0 copy-start.2
  2.2 0.7 copy-done.2
  2.9 0.0 copy-start.3
  2.9 0.7 copy-done.3
  3.7 1.6 %gram_mate.1 = bf16[4,4,144,128]{3,2,1,0:T(8,128)(2,1)S(1)} custom-call(bf16[2,32,128,128]{3,2,1,0:T(8,128)(2,1)S(1)} %copy-done, bf16[2,32,128]{2,1,0:T(8,128)(2,1)S(1)} %copy-done.3, f32[2,16,32]{2,1,0:T(8,128)S(1)} %bitcast.1), custom_call_target="tpu_custom_call" | custom-call | flops 300000000 | bytes 3145728 | tf_op jit(solution)/shard_map/gram_mate/pallas_call | solution.py:84
  5.3 8.7 %collective-permute-start = (bf16[4,4,144,128]{3,2,1,0:T(8,128)(2,1)S(1)}, bf16[4,4,144,128]{3,2,1,0:T(8,128)(2,1)S(1)}, u32[]{:S(2)}, u32[]{:S(2)}) collective-permute-start(bf16[4,4,144,128]{3,2,1,0:T(8,128)(2,1)S(1)} %gram_mate.1), channel_id=1, source_target_pairs={{0,64},{64,0},{128,192},{192,128},{256,320},{320,256},{384,448},{4... | collective-permute-start | bytes 1769480 | tf_op jit(solution)/shard_map/ppermute | solution.py:344
  14.0 1.6 %gram_own.1 = bf16[4,4,144,128]{3,2,1,0:T(8,128)(2,1)S(1)} custom-call(bf16[2,32,128,128]{3,2,1,0:T(8,128)(2,1)S(1)} %copy-done, bf16[2,32,128]{2,1,0:T(8,128)(2,1)S(1)} %copy-done.3, f32[2,16,32]{2,1,0:T(8,128)S(1)} %bitcast.2), custom_call_target="tpu_custom_call" | custom-call | flops 300000000 | bytes 3145728 | tf_op jit(solution)/shard_map/gram_own/pallas_call | solution.py:84
  15.7 0.0 copy-start.5
  15.7 0.0 copy-start.6
  15.7 0.0 collective-permute-done
  15.7 1.0 %add_convert_fusion = bf16[4,4,144,128]{3,2,1,0:T(8,128)(2,1)} fusion(bf16[4,4,144,128]{3,2,1,0:T(8,128)(2,1)S(1)} %collective-permute-done, bf16[4,4,144,128]{3,2,1,0:T(8,128)(2,1)S(1)} %gram_own.1), kind=kLoop, calls=%fused_computation | loop fusion | flops 1179648 | bytes 1769472 | tf_op jit(solution)/shard_map/convert_element_type | solution.py:346
  16.7 3.5 %all-to-all-start = ((bf16[4,4,144,128]{3,2,1,0:T(8,128)(2,1)}), bf16[4,4,144,128]{3,2,1,0:T(8,128)(2,1)S(1)}, u32[]{:S(2)}, u32[]{:S(2)}) async-start(bf16[4,4,144,128]{3,2,1,0:T(8,128)(2,1)} %add_convert_fusion), calls=%async_computation | async-start | bytes 1179648 | tf_op jit(solution)/shard_map/all_to_all | solution.py:334
  20.8 9.3 %all-to-all-done.rx_ref = bf16[4,4,144,128]{3,2,1,0:T(8,128)(2,1)S(1)} async-done(((bf16[4,4,144,128]{3,2,1,0:T(8,128)(2,1)}), bf16[4,4,144,128]{3,2,1,0:T(8,128)(2,1)S(1)}, u32[]{:S(2)}, u32[]{:S(2)}) %all-to-all-start) | async-done | bytes 589856 | tf_op jit(solution)/shard_map/all_to_all | solution.py:334
  30.1 0.0 copy-done.5
  30.1 0.0 copy-done.6
  30.1 3.2 %detect.1 = bf16[8,160,128]{2,1,0:T(8,128)(2,1)S(1)} custom-call(f32[32]{0:T(128)S(1)} %copy-done.6, s32[1]{0:T(128)S(6)} %copy.9.count_ref, bf16[4,4,144,128]{3,2,1,0:T(8,128)(2,1)S(1)} %all-to-all-done.rx_ref, f32[3,2,128,128]{3,2,1,0:T(8,128)S(1)} %copy-done.5), custom_call_target="tpu_custom_call" | custom-call | flops 1000000000 | bytes 4194304 | tf_op jit(solution)/shard_map/detect/pallas_call | solution.py:240
  33.3 0.0 copy-start.1
  33.4 0.0 copy-start.4
  33.4 11.1 %all_to_all.25.fac_ref = bf16[8,160,128]{2,1,0:T(8,128)(2,1)S(1)} all-to-all(bf16[8,160,128]{2,1,0:T(8,128)(2,1)S(1)} %detect.1), channel_id=1, replica_groups=mesh['panel'=8,'sc'=64] {'panel'}, dimensions={0} | all-to-all | bytes 655360 | tf_op jit(solution)/shard_map/all_to_all | solution.py:334
  44.6 11.7 %all_to_all.26 = bf16[8,96,128]{2,1,0:T(8,128)(2,1)S(1)} all-to-all(bf16[8,96,128]{2,1,0:T(8,128)(2,1)S(1)} %broadcast_in_dim.9), channel_id=1, replica_groups={{0,1,2,3,4,5,6,7},{8,9,10,11,12,13,14,15},{16,17,18,19,20,21,22,23},{24..., dimensions={0} | all-to-all | bytes 393216 | tf_op jit(solution)/shard_map/all_to_all | solution.py:334
  56.4 0.7 broadcast_in_dim.10
  57.1 9.1 %all-to-all-start.3 = ((bf16[8,96,128]{2,1,0:T(8,128)(2,1)}), bf16[8,96,128]{2,1,0:T(8,128)(2,1)S(1)}, u32[]{:S(2)}, u32[]{:S(2)}) async-start(bf16[8,96,128]{2,1,0:T(8,128)(2,1)} %broadcast_in_dim.10), calls=%async_computation.3 | async-start | bytes 393216 | tf_op jit(solution)/shard_map/all_to_all | solution.py:334
  66.2 0.0 copy-done.1
  66.2 0.0 copy-done.4
  66.2 8.3 %chain.1 = (bf16[2,32,128,128]{3,2,1,0:T(8,128)(2,1)}, bf16[2,32,128]{2,1,0:T(8,128)(2,1)}) custom-call(bf16[2,32,128,128]{3,2,1,0:T(8,128)(2,1)S(1)} %copy-done.1, bf16[2,32,128]{2,1,0:T(8,128)(2,1)S(1)} %copy-done.4, bf16[8,160,128]{2,1,0:T(8,128)(2,1)S(1)} %all_to_all.25.fac_ref), custom_call_target="tpu_custom_call" | custom-call | flops 1000000000 | bytes 20971520 | tf_op jit(solution)/shard_map/chain/pallas_call | solution.py:292
  74.5 0.4 all-to-all-done.3
  75.0 12.0 %all_to_all.27.in_ref = bf16[8,96,128]{2,1,0:T(8,128)(2,1)S(1)} all-to-all(bf16[8,96,128]{2,1,0:T(8,128)(2,1)S(1)} %broadcast_in_dim.11), channel_id=1, replica_groups=mesh['panel'=8,'sc'=64] {'panel'}, dimensions={0} | all-to-all | bytes 393216 | tf_op jit(solution)/shard_map/all_to_all | solution.py:334
  87.0 0.8 widen.1
  (5 shorter events, 0.1 us)
Async XLA Ops:
  0.6 1.6 %copy-start = (bf16[2,32,128,128]{3,2,1,0:T(8,128)(2,1)S(1)}, bf16[2,32,128,128]{3,2,1,0:T(8,128)(2,1)}, u32[]{:S(2)}) copy-start(bf16[2,32,128,128]{3,2,1,0:T(8,128)(2,1)} %chan_ref.5) | copy-start | bytes 6291460
  2.2 0.7 copy-start.2
  2.9 0.7 copy-start.3
  5.3 10.4 %collective-permute-start = (bf16[4,4,144,128]{3,2,1,0:T(8,128)(2,1)S(1)}, bf16[4,4,144,128]{3,2,1,0:T(8,128)(2,1)S(1)}, u32[]{:S(2)}, u32[]{:S(2)}) collective-permute-start(bf16[4,4,144,128]{3,2,1,0:T(8,128)(2,1)S(1)} %gram_mate.1), channel_id=1, source_target_pairs={{0,64},{64,0},{128,192},{192,128},{256,320},{320,256},{384,448},{4... | collective-permute-start | bytes 1769480 | tf_op jit(solution)/shard_map/ppermute | solution.py:344
  15.7 14.4 %copy-start.5 = (f32[3,2,128,128]{3,2,1,0:T(8,128)S(1)}, f32[3,2,128,128]{3,2,1,0:T(8,128)}, u32[]{:S(2)}) copy-start(f32[3,2,128,128]{3,2,1,0:T(8,128)} %steps_ref.1) | copy-start | bytes 1179652
  15.7 14.4 %copy-start.6 = (f32[32]{0:T(128)S(1)}, f32[32]{0:T(128)}, u32[]{:S(2)}) copy-start(f32[32]{0:T(128)} %noise_ref.1) | copy-start | bytes 388
  16.7 13.4 %all-to-all-start = ((bf16[4,4,144,128]{3,2,1,0:T(8,128)(2,1)}), bf16[4,4,144,128]{3,2,1,0:T(8,128)(2,1)S(1)}, u32[]{:S(2)}, u32[]{:S(2)}) async-start(bf16[4,4,144,128]{3,2,1,0:T(8,128)(2,1)} %add_convert_fusion), calls=%async_computation | async-start | bytes 1179648 | tf_op jit(solution)/shard_map/all_to_all | solution.py:334
  33.3 32.8 %copy-start.1 = (bf16[2,32,128,128]{3,2,1,0:T(8,128)(2,1)S(1)}, bf16[2,32,128,128]{3,2,1,0:T(8,128)(2,1)}, u32[]{:S(2)}) copy-start(bf16[2,32,128,128]{3,2,1,0:T(8,128)(2,1)} %chan_ref.5) | copy-start | bytes 6291460
  33.4 32.8 %copy-start.4 = (bf16[2,32,128]{2,1,0:T(8,128)(2,1)S(1)}, bf16[2,32,128]{2,1,0:T(8,128)(2,1)}, u32[]{:S(2)}) copy-start(bf16[2,32,128]{2,1,0:T(8,128)(2,1)} %recv_ref.5) | copy-start | bytes 49156
  57.1 17.8 %all-to-all-start.3 = ((bf16[8,96,128]{2,1,0:T(8,128)(2,1)}), bf16[8,96,128]{2,1,0:T(8,128)(2,1)S(1)}, u32[]{:S(2)}, u32[]{:S(2)}) async-start(bf16[8,96,128]{2,1,0:T(8,128)(2,1)} %broadcast_in_dim.10), calls=%async_computation.3 | async-start | bytes 393216 | tf_op jit(solution)/shard_map/all_to_all | solution.py:334

commit v3 on v2

--- a/solution.py
+++ b/solution.py
@@ -61,7 +61,7 @@
     at = iota((8, 2 * U), 0)
     for j in range(SUB):
         row = core * SUB + j
-        h_re, h_im = chan_ref[0, row], chan_ref[1, row]
+        h_re, h_im = chan_ref[0, j], chan_ref[1, j]
         stack = jnp.concatenate([h_re, h_im], axis=0)
         other = jnp.concatenate([h_im, -h_re], axis=0)
         both = jnp.concatenate([stack, other], axis=1)
@@ -81,18 +81,21 @@
 
 
 def gram_call(own, channel, received, cot):
+    def place(i):
+        core = lax.rem(lax.axis_index("panel") + (0 if own else 1), 2)
+        return (0, 2 * i + core, 0, 0)
+
     return pl.pallas_call(
         functools.partial(gram_kernel, own),
         grid=(4,),
         out_shape=jax.ShapeDtypeStruct((NP // 2, SUB, ROWS, U), BF16),
         in_specs=[
-            pl.BlockSpec((2, 8, A, U), lambda i: (0, i, 0, 0)),
+            pl.BlockSpec((2, SUB, A, U), place),
             pl.BlockSpec((2, 8, A), lambda i: (0, i, 0)),
             pl.BlockSpec((2, 16, 32), lambda i: (0, 0, 0)),
         ],
         out_specs=pl.BlockSpec((1, SUB, ROWS, U), lambda i: (i, 0, 0, 0)),
         scratch_shapes=[pltpu.VMEM((4, 32, U), F32)],
-        compiler_params=pltpu.CompilerParams(vmem_limit_bytes=8 << 20),
         cost_estimate=pl.CostEstimate(flops=3 * 10**8, bytes_accessed=3 << 20, transcendentals=0),
         name="gram_own" if own else "gram_mate",
     )(channel, received, cot)
@@ -252,7 +255,8 @@
     )(noise, counts, rx, steps)
 
 
-def chain_kernel(chan_ref, recv_ref, fac_ref, gchan_ref, grecv_ref):
+def chain_kernel(chan_ref, recv_ref, fac_ref, *rest):
+    gchan_ref, grecv_ref = rest[-2:]
     at = iota((8, U), 0)
     even = iota((16, U), 0) % 2 == 0
     gy_re = jnp.zeros((8, A), F32)
@@ -288,27 +292,24 @@
     grecv_ref[1] = gy_im.astype(BF16)
 
 
-def chain_call(channel, received, factors):
+def chain_call(half, channel, received, factors, earlier=()):
+    wide = pl.BlockSpec((2, 8, A, U), lambda i: (0, i + 2 * half, 0, 0))
+    flat = pl.BlockSpec((2, 8, A), lambda i: (0, i + 2 * half, 0))
     return pl.pallas_call(
         chain_kernel,
-        grid=(4,),
+        grid=(2,),
         out_shape=(
             jax.ShapeDtypeStruct((2, 32, A, U), BF16),
             jax.ShapeDtypeStruct((2, 32, A), BF16),
         ),
-        in_specs=[
-            pl.BlockSpec((2, 8, A, U), lambda i: (0, i, 0, 0)),
-            pl.BlockSpec((2, 8, A), lambda i: (0, i, 0)),
-            pl.BlockSpec((2, 64, U), lambda i: (i, 0, 0)),
-        ],
-        out_specs=(
-            pl.BlockSpec((2, 8, A, U), lambda i: (0, i, 0, 0)),
-            pl.BlockSpec((2, 8, A), lambda i: (0, i, 0)),
-        ),
+        in_specs=[wide, flat, pl.BlockSpec((2, 64, U), lambda i: (i + 2 * half, 0, 0))]
+        + [pl.BlockSpec(memory_space=pl.ANY)] * len(earlier),
+        out_specs=(wide, flat),
+        input_output_aliases={3: 0, 4: 1} if earlier else {},
         compiler_params=pltpu.CompilerParams(vmem_limit_bytes=8 << 20),
-        cost_estimate=pl.CostEstimate(flops=10**9, bytes_accessed=20 << 20, transcendentals=0),
-        name="chain",
-    )(channel, received, factors)
+        cost_estimate=pl.CostEstimate(flops=10**9, bytes_accessed=12 << 20, transcendentals=0),
+        name="chain_b" if earlier else "chain_a",
+    )(channel, received, factors, *earlier)
 
 
 def widen_kernel(in_ref, out_ref):
@@ -347,11 +348,13 @@
     rx = exchange(pair, "panel", [[0, 2, 4, 6], [1, 3, 5, 7]])
     both = exchange(detect_call(noise, counts, rx, steps), "panel")
     part = jnp.sum(both[:, 64:].astype(F32), axis=0).astype(BF16)
-    grad_channel, grad_received = chain_call(channel, received, both)
-    for groups in (y_groups, z_groups):
+    grads = ()
+    for half, groups in enumerate((y_groups, z_groups)):
+        grads = chain_call(half, channel, received, both, grads)
         every = exchange(jnp.broadcast_to(part, (8, 96, U)), "sc", groups)
         part = jnp.sum(every.astype(F32), axis=0).astype(BF16)
-    part, grad_received = lax.optimization_barrier((part, grad_received))
+        part, grads = lax.optimization_barrier((part, grads))
+    grad_channel, grad_received = grads
     every = exchange(jnp.broadcast_to(part, (8, 96, U)), "panel")
     return (grad_channel, grad_received, widen_call(every))
 

time: 88.3 us -> 92 us (1.042)
  blocking collectives: 34.9 us -> 22.7 us
  waiting for transfers between devices: 9.7 us -> 18.4 us
  Pallas kernels: 15.5 us -> 21.2 us
  starting transfers between devices: 21.3 us -> 24 us
  local copies, waits for them, and re-layouts: 3.8 us -> 1.45 us
  other arithmetic: 1.06 us -> 2.18 us
    all_to_all x3 -> x2, blocking collectives: 34.9 us -> 22.7 us  [exchange(): lax.all_to_all(value, axis, split_axis=0, concat_axis=0, tiled=True, axis...]
    all_to_all x2 -> x3, waiting for transfers between devices: 9.7 us -> 18.4 us  [exchange(): lax.all_to_all(value, axis, split_axis=0, concat_axis=0, tiled=True, axis...]
    pallas_call x2, Pallas kernels: 3.25 us -> 8.13 us  [gram_call(): pl.pallas_call(functools.partial(gram_kernel, own), grid=(4,), out_shape=...]
    unnamed x14 -> x8, local copies, waits for them, and re-layouts: 3.05 us -> 0.02 us
    all_to_all x2 -> x3, starting transfers between devices: 12.6 us -> 15.3 us  [exchange(): lax.all_to_all(value, axis, split_axis=0, concat_axis=0, tiled=True, axis...]
    convert_element_type x1, other arithmetic: 0.97 us -> 2.08 us  [on_device(): pair = (own.astype(F32) + got.astype(F32)).astype(BF16)]
    pallas_call x1 -> x2, Pallas kernels: 8.3 us -> 9.11 us  [chain_call(): pl.pallas_call(chain_kernel, grid=(2,), out_shape=(jax.ShapeDtypeStruct((...]
  transfers between devices with their start and end apart: 3 -> 4, of which waited for: 2 -> 3; matrix products, arithmetic and copies ran while one was open for 0% -> 0% of each run, Pallas kernels for 11% -> 14%
where the time goes in v3:
time: 92 us; the launch traced here: 91.4 us
  starting transfers between devices  24 us (26%)
  blocking collectives  22.7 us (25%)
  Pallas kernels  21.2 us (23%)
  waiting for transfers between devices  18.4 us (20%)
  other arithmetic  2.18 us (2%)
  local copies, waits for them, and re-layouts  1.45 us (2%)
  between operations  1.37 us (1%)
    all_to_all x2, blocking collectives, exchange(): lax.all_to_all(value, axis, split_axis=0, concat_axis=0, tiled=True, axis...  22.7 us
    all_to_all x3, waiting for transfers between devices, exchange(): lax.all_to_all(value, axis, split_axis=0, concat_axis=0, tiled=True, axis...  18.4 us
    all_to_all x3, starting transfers between devices, exchange(): lax.all_to_all(value, axis, split_axis=0, concat_axis=0, tiled=True, axis...  15.3 us
    pallas_call x2, Pallas kernels, chain_call(): pl.pallas_call(chain_kernel, grid=(2,), out_shape=(jax.ShapeDtypeStruct((...  9.11 us
    ppermute x1, starting transfers between devices, on_device(): got = lax.ppermute(away, 'panel', [(p, p ^ 1) for p in range(NP)])  8.73 us
    pallas_call x2, Pallas kernels, gram_call(): pl.pallas_call(functools.partial(gram_kernel, own), grid=(4,), out_shape=...  8.13 us
    pallas_call x1, Pallas kernels, detect_call(): pl.pallas_call(detect_kernel, out_shape=jax.ShapeDtypeStruct((NP, 160, U)...  3.23 us
    convert_element_type x1, other arithmetic, on_device(): pair = (own.astype(F32) + got.astype(F32)).astype(BF16)  2.08 us
  transfers between devices with their start and end apart: 4, of which 3 were waited for; matrix products, arithmetic and copies ran while one was open for 0% of the time, Pallas kernels for 14%

profile of v3, /device:TPU:1, one launch (start us, length us, event | category | flops | bytes accessed | tf_op | source)
XLA Modules:
  0.0 91.4 jit_solution(16755105296314838409)
XLA Ops:
  0.6 4.1 %gram_mate.1 = bf16[4,4,144,128]{3,2,1,0:T(8,128)(2,1)} custom-call(bf16[2,32,128,128]{3,2,1,0:T(8,128)(2,1)} %chan_ref.7, bf16[2,32,128]{2,1,0:T(8,128)(2,1)} %recv_ref.7, f32[2,16,32]{2,1,0:T(8,128)} %bitcast.1), custom_call_target="tpu_custom_call" | custom-call | flops 300000000 | bytes 3145728 | tf_op jit(solution)/shard_map/gram_mate/pallas_call | solution.py:88
  4.7 8.7 %collective-permute-start = (bf16[4,4,144,128]{3,2,1,0:T(8,128)(2,1)}, bf16[4,4,144,128]{3,2,1,0:T(8,128)(2,1)S(1)}, u32[]{:S(2)}, u32[]{:S(2)}) collective-permute-start(bf16[4,4,144,128]{3,2,1,0:T(8,128)(2,1)} %gram_mate.1), channel_id=1, source_target_pairs={{0,64},{64,0},{128,192},{192,128},{256,320},{320,256},{384,448},{4... | collective-permute-start | bytes 1769480 | tf_op jit(solution)/shard_map/ppermute | solution.py:345
  13.4 4.1 %gram_own.1 = bf16[4,4,144,128]{3,2,1,0:T(8,128)(2,1)} custom-call(bf16[2,32,128,128]{3,2,1,0:T(8,128)(2,1)} %chan_ref.7, bf16[2,32,128]{2,1,0:T(8,128)(2,1)} %recv_ref.7, f32[2,16,32]{2,1,0:T(8,128)} %bitcast.2), custom_call_target="tpu_custom_call" | custom-call | flops 300000000 | bytes 3145728 | tf_op jit(solution)/shard_map/gram_own/pallas_call | solution.py:88
  17.5 0.0 copy-start.2
  17.5 0.0 copy-start.3
  17.5 0.0 collective-permute-done
  17.5 2.1 %add_convert_fusion = bf16[4,4,144,128]{3,2,1,0:T(8,128)(2,1)} fusion(bf16[4,4,144,128]{3,2,1,0:T(8,128)(2,1)S(1)} %collective-permute-done, bf16[4,4,144,128]{3,2,1,0:T(8,128)(2,1)} %gram_own.1), kind=kLoop, calls=%fused_computation | loop fusion | flops 1179648 | bytes 1769472 | tf_op jit(solution)/shard_map/convert_element_type | solution.py:347
  19.6 3.5 %all-to-all-start = ((bf16[4,4,144,128]{3,2,1,0:T(8,128)(2,1)}), bf16[4,4,144,128]{3,2,1,0:T(8,128)(2,1)S(1)}, u32[]{:S(2)}, u32[]{:S(2)}) async-start(bf16[4,4,144,128]{3,2,1,0:T(8,128)(2,1)} %add_convert_fusion), calls=%async_computation | async-start | bytes 1179648 | tf_op jit(solution)/shard_map/all_to_all | solution.py:335
  23.7 0.0 copy-start
  23.7 0.0 copy-start.1
  23.8 9.6 %all-to-all-done.rx_ref = bf16[4,4,144,128]{3,2,1,0:T(8,128)(2,1)S(1)} async-done(((bf16[4,4,144,128]{3,2,1,0:T(8,128)(2,1)}), bf16[4,4,144,128]{3,2,1,0:T(8,128)(2,1)S(1)}, u32[]{:S(2)}, u32[]{:S(2)}) %all-to-all-start) | async-done | bytes 589856 | tf_op jit(solution)/shard_map/all_to_all | solution.py:335
  33.3 0.0 copy-done.2
  33.3 0.0 copy-done.3
  33.3 3.2 %detect.1 = bf16[8,160,128]{2,1,0:T(8,128)(2,1)S(1)} custom-call(f32[32]{0:T(128)S(1)} %copy-done.3, s32[1]{0:T(128)S(6)} %copy.13.count_ref, bf16[4,4,144,128]{3,2,1,0:T(8,128)(2,1)S(1)} %all-to-all-done.rx_ref, f32[3,2,128,128]{3,2,1,0:T(8,128)S(1)} %copy-done.2), custom_call_target="tpu_custom_call" | custom-call | flops 1000000000 | bytes 4194304 | tf_op jit(solution)/shard_map/detect/pallas_call | solution.py:243
  36.6 10.7 %all_to_all.25.fac_ref = bf16[8,160,128]{2,1,0:T(8,128)(2,1)S(1)} all-to-all(bf16[8,160,128]{2,1,0:T(8,128)(2,1)S(1)} %detect.1), channel_id=1, replica_groups=mesh['panel'=8,'sc'=64] {'panel'}, dimensions={0} | all-to-all | bytes 655360 | tf_op jit(solution)/shard_map/all_to_all | solution.py:335
  47.3 0.7 broadcast_in_dim.9
  48.0 3.4 %all-to-all-start.2 = ((bf16[8,96,128]{2,1,0:T(8,128)(2,1)}), bf16[8,96,128]{2,1,0:T(8,128)(2,1)S(1)}, u32[]{:S(2)}, u32[]{:S(2)}) async-start(bf16[8,96,128]{2,1,0:T(8,128)(2,1)} %broadcast_in_dim.9), calls=%async_computation.2 | async-start | bytes 393216 | tf_op jit(solution)/shard_map/all_to_all | solution.py:335
  51.4 0.0 copy-done
  51.4 0.0 copy-done.1
  51.4 4.6 %chain_a.1 = (bf16[2,32,128,128]{3,2,1,0:T(8,128)(2,1)}, bf16[2,32,128]{2,1,0:T(8,128)(2,1)}) custom-call(bf16[2,32,128,128]{3,2,1,0:T(8,128)(2,1)S(1)} %copy-done, bf16[2,32,128]{2,1,0:T(8,128)(2,1)S(1)} %copy-done.1, bf16[8,160,128]{2,1,0:T(8,128)(2,1)S(1)} %all_to_all.25.fac_ref), custom_call_target="tpu_custom_call" | custom-call | flops 1000000000 | bytes 12582912 | tf_op jit(solution)/shard_map/chain_a/pallas_call | solution.py:298
  56.0 4.7 %all-to-all-done.2 = bf16[8,96,128]{2,1,0:T(8,128)(2,1)S(1)} async-done(((bf16[8,96,128]{2,1,0:T(8,128)(2,1)}), bf16[8,96,128]{2,1,0:T(8,128)(2,1)S(1)}, u32[]{:S(2)}, u32[]{:S(2)}) %all-to-all-start.2) | async-done | bytes 196640 | tf_op jit(solution)/shard_map/all_to_all | solution.py:335
  60.7 0.7 broadcast_in_dim.10
  61.4 8.4 %all-to-all-start.3 = ((bf16[8,96,128]{2,1,0:T(8,128)(2,1)}), bf16[8,96,128]{2,1,0:T(8,128)(2,1)S(1)}, u32[]{:S(2)}, u32[]{:S(2)}) async-start(bf16[8,96,128]{2,1,0:T(8,128)(2,1)} %broadcast_in_dim.10), calls=%async_computation.3 | async-start | bytes 393216 | tf_op jit(solution)/shard_map/all_to_all | solution.py:335
  69.8 4.6 %chain_b.1 = (bf16[2,32,128,128]{3,2,1,0:T(8,128)(2,1)}, bf16[2,32,128]{2,1,0:T(8,128)(2,1)}) custom-call(bf16[2,32,128,128]{3,2,1,0:T(8,128)(2,1)S(1)} %copy-done, bf16[2,32,128]{2,1,0:T(8,128)(2,1)S(1)} %copy-done.1, bf16[8,160,128]{2,1,0:T(8,128)(2,1)S(1)} %all_to_all.25.fac_ref, ...), custom_call_target="tpu_custom_call", output_to_operand_aliasing={{0}: (3, {}), {1}: (4, {})} | custom-call | flops 1000000000 | bytes 12582912 | tf_op jit(solution)/shard_map/chain_b/pallas_call | solution.py:298
  74.3 4.2 %all-to-all-done.3 = bf16[8,96,128]{2,1,0:T(8,128)(2,1)S(1)} async-done(((bf16[8,96,128]{2,1,0:T(8,128)(2,1)}), bf16[8,96,128]{2,1,0:T(8,128)(2,1)S(1)}, u32[]{:S(2)}, u32[]{:S(2)}) %all-to-all-start.3) | async-done | bytes 196640 | tf_op jit(solution)/shard_map/all_to_all | solution.py:335
  78.6 12.0 %all_to_all.26.in_ref = bf16[8,96,128]{2,1,0:T(8,128)(2,1)S(1)} all-to-all(bf16[8,96,128]{2,1,0:T(8,128)(2,1)S(1)} %broadcast_in_dim.11), channel_id=1, replica_groups=mesh['panel'=8,'sc'=64] {'panel'}, dimensions={0} | all-to-all | bytes 393216 | tf_op jit(solution)/shard_map/all_to_all | solution.py:335
  90.6 0.8 widen.1
  (4 shorter events, 0.1 us)
Async XLA Ops:
  4.7 12.8 %collective-permute-start = (bf16[4,4,144,128]{3,2,1,0:T(8,128)(2,1)}, bf16[4,4,144,128]{3,2,1,0:T(8,128)(2,1)S(1)}, u32[]{:S(2)}, u32[]{:S(2)}) collective-permute-start(bf16[4,4,144,128]{3,2,1,0:T(8,128)(2,1)} %gram_mate.1), channel_id=1, source_target_pairs={{0,64},{64,0},{128,192},{192,128},{256,320},{320,256},{384,448},{4... | collective-permute-start | bytes 1769480 | tf_op jit(solution)/shard_map/ppermute | solution.py:345
  17.5 15.8 %copy-start.2 = (f32[3,2,128,128]{3,2,1,0:T(8,128)S(1)}, f32[3,2,128,128]{3,2,1,0:T(8,128)}, u32[]{:S(2)}) copy-start(f32[3,2,128,128]{3,2,1,0:T(8,128)} %steps_ref.1) | copy-start | bytes 1179652
  17.5 15.8 %copy-start.3 = (f32[32]{0:T(128)S(1)}, f32[32]{0:T(128)}, u32[]{:S(2)}) copy-start(f32[32]{0:T(128)} %noise_ref.1) | copy-start | bytes 388
  19.6 13.7 %all-to-all-start = ((bf16[4,4,144,128]{3,2,1,0:T(8,128)(2,1)}), bf16[4,4,144,128]{3,2,1,0:T(8,128)(2,1)S(1)}, u32[]{:S(2)}, u32[]{:S(2)}) async-start(bf16[4,4,144,128]{3,2,1,0:T(8,128)(2,1)} %add_convert_fusion), calls=%async_computation | async-start | bytes 1179648 | tf_op jit(solution)/shard_map/all_to_all | solution.py:335
  23.7 27.7 %copy-start = (bf16[2,32,128,128]{3,2,1,0:T(8,128)(2,1)S(1)}, bf16[2,32,128,128]{3,2,1,0:T(8,128)(2,1)}, u32[]{:S(2)}) copy-start(bf16[2,32,128,128]{3,2,1,0:T(8,128)(2,1)} %chan_ref.7) | copy-start | bytes 6291460
  23.7 27.7 %copy-start.1 = (bf16[2,32,128]{2,1,0:T(8,128)(2,1)S(1)}, bf16[2,32,128]{2,1,0:T(8,128)(2,1)}, u32[]{:S(2)}) copy-start(bf16[2,32,128]{2,1,0:T(8,128)(2,1)} %recv_ref.7) | copy-start | bytes 49156
  48.0 12.7 %all-to-all-start.2 = ((bf16[8,96,128]{2,1,0:T(8,128)(2,1)}), bf16[8,96,128]{2,1,0:T(8,128)(2,1)S(1)}, u32[]{:S(2)}, u32[]{:S(2)}) async-start(bf16[8,96,128]{2,1,0:T(8,128)(2,1)} %broadcast_in_dim.9), calls=%async_computation.2 | async-start | bytes 393216 | tf_op jit(solution)/shard_map/all_to_all | solution.py:335
  61.4 17.1 %all-to-all-start.3 = ((bf16[8,96,128]{2,1,0:T(8,128)(2,1)}), bf16[8,96,128]{2,1,0:T(8,128)(2,1)S(1)}, u32[]{:S(2)}, u32[]{:S(2)}) async-start(bf16[8,96,128]{2,1,0:T(8,128)(2,1)} %broadcast_in_dim.10), calls=%async_computation.3 | async-start | bytes 393216 | tf_op jit(solution)/shard_map/all_to_all | solution.py:335

commit v4 on v3

--- a/solution.py
+++ b/solution.py
@@ -61,7 +61,7 @@
     at = iota((8, 2 * U), 0)
     for j in range(SUB):
         row = core * SUB + j
-        h_re, h_im = chan_ref[0, j], chan_ref[1, j]
+        h_re, h_im = chan_ref[0, row], chan_ref[1, row]
         stack = jnp.concatenate([h_re, h_im], axis=0)
         other = jnp.concatenate([h_im, -h_re], axis=0)
         both = jnp.concatenate([stack, other], axis=1)
@@ -81,21 +81,18 @@
 
 
 def gram_call(own, channel, received, cot):
-    def place(i):
-        core = lax.rem(lax.axis_index("panel") + (0 if own else 1), 2)
-        return (0, 2 * i + core, 0, 0)
-
     return pl.pallas_call(
         functools.partial(gram_kernel, own),
         grid=(4,),
         out_shape=jax.ShapeDtypeStruct((NP // 2, SUB, ROWS, U), BF16),
         in_specs=[
-            pl.BlockSpec((2, SUB, A, U), place),
+            pl.BlockSpec((2, 8, A, U), lambda i: (0, i, 0, 0)),
             pl.BlockSpec((2, 8, A), lambda i: (0, i, 0)),
             pl.BlockSpec((2, 16, 32), lambda i: (0, 0, 0)),
         ],
         out_specs=pl.BlockSpec((1, SUB, ROWS, U), lambda i: (i, 0, 0, 0)),
         scratch_shapes=[pltpu.VMEM((4, 32, U), F32)],
+        compiler_params=pltpu.CompilerParams(vmem_limit_bytes=8 << 20),
         cost_estimate=pl.CostEstimate(flops=3 * 10**8, bytes_accessed=3 << 20, transcendentals=0),
         name="gram_own" if own else "gram_mate",
     )(channel, received, cot)

time: 92 us -> 89.1 us (0.968)
  Pallas kernels: 21.2 us -> 16.4 us
  local copies, waits for them, and re-layouts: 1.45 us -> 4.48 us
  other arithmetic: 2.18 us -> 1.06 us
    pallas_call x2, Pallas kernels: 8.13 us -> 3.25 us  [gram_call(): pl.pallas_call(functools.partial(gram_kernel, own), grid=(4,), out_shape=...]
    unnamed x8 -> x14, local copies, waits for them, and re-layouts: 0.02 us -> 3.05 us
    convert_element_type x1, other arithmetic: 2.08 us -> 0.97 us  [on_device(): pair = (own.astype(F32) + got.astype(F32)).astype(BF16)]
  transfers between devices with their start and end apart: 4 -> 4, of which waited for: 3 -> 3; matrix products, arithmetic and copies ran while one was open for 0% -> 0% of each run, Pallas kernels for 14% -> 12%
where the time goes in v4:
time: 89.1 us; the launch traced here: 88.5 us
  starting transfers between devices  24 us (27%)
  blocking collectives  23 us (26%)
  waiting for transfers between devices  18.1 us (20%)
  Pallas kernels  16.4 us (18%)
  local copies, waits for them, and re-layouts  4.48 us (5%)
  between operations  1.41 us (2%)
  other arithmetic  1.06 us (1%)
    all_to_all x2, blocking collectives, exchange(): lax.all_to_all(value, axis, split_axis=0, concat_axis=0, tiled=True, axis...  23 us
    all_to_all x3, waiting for transfers between devices, exchange(): lax.all_to_all(value, axis, split_axis=0, concat_axis=0, tiled=True, axis...  18.1 us
    all_to_all x3, starting transfers between devices, exchange(): lax.all_to_all(value, axis, split_axis=0, concat_axis=0, tiled=True, axis...  15.3 us
    pallas_call x2, Pallas kernels, chain_call(): pl.pallas_call(chain_kernel, grid=(2,), out_shape=(jax.ShapeDtypeStruct((...  9.11 us
    ppermute x1, starting transfers between devices, on_device(): got = lax.ppermute(away, 'panel', [(p, p ^ 1) for p in range(NP)])  8.75 us
    pallas_call x2, Pallas kernels, gram_call(): pl.pallas_call(functools.partial(gram_kernel, own), grid=(4,), out_shape=...  3.25 us
    pallas_call x1, Pallas kernels, detect_call(): pl.pallas_call(detect_kernel, out_shape=jax.ShapeDtypeStruct((NP, 160, U)...  3.23 us
    unnamed x14, local copies, waits for them, and re-layouts  3.05 us
  transfers between devices with their start and end apart: 4, of which 3 were waited for; matrix products, arithmetic and copies ran while one was open for 0% of the time, Pallas kernels for 12%

profile of v4, /device:TPU:1, one launch (start us, length us, event | category | flops | bytes accessed | tf_op | source)
XLA Modules:
  0.0 88.5 jit_solution(12118863844039673345)
XLA Ops:
  0.6 0.0 copy-start
  0.6 1.6 %copy-done = bf16[2,32,128,128]{3,2,1,0:T(8,128)(2,1)S(1)} copy-done((bf16[2,32,128,128]{3,2,1,0:T(8,128)(2,1)S(1)}, bf16[2,32,128,128]{3,2,1,0:T(8,128)(2,1)}, u32[]{:S(2)}) %copy-start) | copy-done | bytes 2097176
  2.2 0.0 copy-start.2
  2.2 0.7 copy-done.2
  2.9 0.0 copy-start.4
  2.9 0.7 copy-done.4
  3.7 1.6 %gram_mate.1 = bf16[4,4,144,128]{3,2,1,0:T(8,128)(2,1)S(1)} custom-call(bf16[2,32,128,128]{3,2,1,0:T(8,128)(2,1)S(1)} %copy-done, bf16[2,32,128]{2,1,0:T(8,128)(2,1)S(1)} %copy-done.2, f32[2,16,32]{2,1,0:T(8,128)S(1)} %bitcast.1), custom_call_target="tpu_custom_call" | custom-call | flops 300000000 | bytes 3145728 | tf_op jit(solution)/shard_map/gram_mate/pallas_call | solution.py:84
  5.3 8.7 %collective-permute-start = (bf16[4,4,144,128]{3,2,1,0:T(8,128)(2,1)S(1)}, bf16[4,4,144,128]{3,2,1,0:T(8,128)(2,1)S(1)}, u32[]{:S(2)}, u32[]{:S(2)}) collective-permute-start(bf16[4,4,144,128]{3,2,1,0:T(8,128)(2,1)S(1)} %gram_mate.1), channel_id=1, source_target_pairs={{0,64},{64,0},{128,192},{192,128},{256,320},{320,256},{384,448},{4... | collective-permute-start | bytes 1769480 | tf_op jit(solution)/shard_map/ppermute | solution.py:342
  14.0 1.6 %gram_own.1 = bf16[4,4,144,128]{3,2,1,0:T(8,128)(2,1)S(1)} custom-call(bf16[2,32,128,128]{3,2,1,0:T(8,128)(2,1)S(1)} %copy-done, bf16[2,32,128]{2,1,0:T(8,128)(2,1)S(1)} %copy-done.2, f32[2,16,32]{2,1,0:T(8,128)S(1)} %bitcast.2), custom_call_target="tpu_custom_call" | custom-call | flops 300000000 | bytes 3145728 | tf_op jit(solution)/shard_map/gram_own/pallas_call | solution.py:84
  15.7 0.0 copy-start.5
  15.7 0.0 copy-start.6
  15.7 0.0 collective-permute-done
  15.7 1.0 %add_convert_fusion = bf16[4,4,144,128]{3,2,1,0:T(8,128)(2,1)} fusion(bf16[4,4,144,128]{3,2,1,0:T(8,128)(2,1)S(1)} %collective-permute-done, bf16[4,4,144,128]{3,2,1,0:T(8,128)(2,1)S(1)} %gram_own.1), kind=kLoop, calls=%fused_computation | loop fusion | flops 1179648 | bytes 1769472 | tf_op jit(solution)/shard_map/convert_element_type | solution.py:344
  16.7 3.5 %all-to-all-start = ((bf16[4,4,144,128]{3,2,1,0:T(8,128)(2,1)}), bf16[4,4,144,128]{3,2,1,0:T(8,128)(2,1)S(1)}, u32[]{:S(2)}, u32[]{:S(2)}) async-start(bf16[4,4,144,128]{3,2,1,0:T(8,128)(2,1)} %add_convert_fusion), calls=%async_computation | async-start | bytes 1179648 | tf_op jit(solution)/shard_map/all_to_all | solution.py:332
  20.8 0.0 copy-start.1
  20.8 0.0 copy-start.3
  20.8 9.3 %all-to-all-done.rx_ref = bf16[4,4,144,128]{3,2,1,0:T(8,128)(2,1)S(1)} async-done(((bf16[4,4,144,128]{3,2,1,0:T(8,128)(2,1)}), bf16[4,4,144,128]{3,2,1,0:T(8,128)(2,1)S(1)}, u32[]{:S(2)}, u32[]{:S(2)}) %all-to-all-start) | async-done | bytes 589856 | tf_op jit(solution)/shard_map/all_to_all | solution.py:332
  30.1 0.0 copy-done.5
  30.1 0.0 copy-done.6
  30.1 3.2 %detect.1 = bf16[8,160,128]{2,1,0:T(8,128)(2,1)S(1)} custom-call(f32[32]{0:T(128)S(1)} %copy-done.6, s32[1]{0:T(128)S(6)} %copy.13.count_ref, bf16[4,4,144,128]{3,2,1,0:T(8,128)(2,1)S(1)} %all-to-all-done.rx_ref, f32[3,2,128,128]{3,2,1,0:T(8,128)S(1)} %copy-done.5), custom_call_target="tpu_custom_call" | custom-call | flops 1000000000 | bytes 4194304 | tf_op jit(solution)/shard_map/detect/pallas_call | solution.py:240
  33.3 11.0 %all_to_all.25.fac_ref = bf16[8,160,128]{2,1,0:T(8,128)(2,1)S(1)} all-to-all(bf16[8,160,128]{2,1,0:T(8,128)(2,1)S(1)} %detect.1), channel_id=1, replica_groups=mesh['panel'=8,'sc'=64] {'panel'}, dimensions={0} | all-to-all | bytes 655360 | tf_op jit(solution)/shard_map/all_to_all | solution.py:332
  44.4 0.7 broadcast_in_dim.9
  45.1 3.4 %all-to-all-start.2 = ((bf16[8,96,128]{2,1,0:T(8,128)(2,1)}), bf16[8,96,128]{2,1,0:T(8,128)(2,1)S(1)}, u32[]{:S(2)}, u32[]{:S(2)}) async-start(bf16[8,96,128]{2,1,0:T(8,128)(2,1)} %broadcast_in_dim.9), calls=%async_computation.2 | async-start | bytes 393216 | tf_op jit(solution)/shard_map/all_to_all | solution.py:332
  48.5 0.0 copy-done.1
  48.5 0.0 copy-done.3
  48.5 4.6 %chain_a.1 = (bf16[2,32,128,128]{3,2,1,0:T(8,128)(2,1)}, bf16[2,32,128]{2,1,0:T(8,128)(2,1)}) custom-call(bf16[2,32,128,128]{3,2,1,0:T(8,128)(2,1)S(1)} %copy-done.1, bf16[2,32,128]{2,1,0:T(8,128)(2,1)S(1)} %copy-done.3, bf16[8,160,128]{2,1,0:T(8,128)(2,1)S(1)} %all_to_all.25.fac_ref), custom_call_target="tpu_custom_call" | custom-call | flops 1000000000 | bytes 12582912 | tf_op jit(solution)/shard_map/chain_a/pallas_call | solution.py:295
  53.1 4.7 %all-to-all-done.2 = bf16[8,96,128]{2,1,0:T(8,128)(2,1)S(1)} async-done(((bf16[8,96,128]{2,1,0:T(8,128)(2,1)}), bf16[8,96,128]{2,1,0:T(8,128)(2,1)S(1)}, u32[]{:S(2)}, u32[]{:S(2)}) %all-to-all-start.2) | async-done | bytes 196640 | tf_op jit(solution)/shard_map/all_to_all | solution.py:332
  57.8 0.7 broadcast_in_dim.10
  58.5 8.4 %all-to-all-start.3 = ((bf16[8,96,128]{2,1,0:T(8,128)(2,1)}), bf16[8,96,128]{2,1,0:T(8,128)(2,1)S(1)}, u32[]{:S(2)}, u32[]{:S(2)}) async-start(bf16[8,96,128]{2,1,0:T(8,128)(2,1)} %broadcast_in_dim.10), calls=%async_computation.3 | async-start | bytes 393216 | tf_op jit(solution)/shard_map/all_to_all | solution.py:332
  66.9 4.6 %chain_b.1 = (bf16[2,32,128,128]{3,2,1,0:T(8,128)(2,1)}, bf16[2,32,128]{2,1,0:T(8,128)(2,1)}) custom-call(bf16[2,32,128,128]{3,2,1,0:T(8,128)(2,1)S(1)} %copy-done.1, bf16[2,32,128]{2,1,0:T(8,128)(2,1)S(1)} %copy-done.3, bf16[8,160,128]{2,1,0:T(8,128)(2,1)S(1)} %all_to_all.25.fac_ref, ...), custom_call_target="tpu_custom_call", output_to_operand_aliasing={{0}: (3, {}), {1}: (4, {})} | custom-call | flops 1000000000 | bytes 12582912 | tf_op jit(solution)/shard_map/chain_b/pallas_call | solution.py:295
  71.4 4.2 %all-to-all-done.3 = bf16[8,96,128]{2,1,0:T(8,128)(2,1)S(1)} async-done(((bf16[8,96,128]{2,1,0:T(8,128)(2,1)}), bf16[8,96,128]{2,1,0:T(8,128)(2,1)S(1)}, u32[]{:S(2)}, u32[]{:S(2)}) %all-to-all-start.3) | async-done | bytes 196640 | tf_op jit(solution)/shard_map/all_to_all | solution.py:332
  75.7 12.0 %all_to_all.26.in_ref = bf16[8,96,128]{2,1,0:T(8,128)(2,1)S(1)} all-to-all(bf16[8,96,128]{2,1,0:T(8,128)(2,1)S(1)} %broadcast_in_dim.11), channel_id=1, replica_groups=mesh['panel'=8,'sc'=64] {'panel'}, dimensions={0} | all-to-all | bytes 393216 | tf_op jit(solution)/shard_map/all_to_all | solution.py:332
  87.7 0.8 widen.1
  (4 shorter events, 0.1 us)
Async XLA Ops:
  0.6 1.6 %copy-start = (bf16[2,32,128,128]{3,2,1,0:T(8,128)(2,1)S(1)}, bf16[2,32,128,128]{3,2,1,0:T(8,128)(2,1)}, u32[]{:S(2)}) copy-start(bf16[2,32,128,128]{3,2,1,0:T(8,128)(2,1)} %chan_ref.7) | copy-start | bytes 6291460
  2.2 0.7 copy-start.2
  2.9 0.7 copy-start.4
  5.3 10.4 %collective-permute-start = (bf16[4,4,144,128]{3,2,1,0:T(8,128)(2,1)S(1)}, bf16[4,4,144,128]{3,2,1,0:T(8,128)(2,1)S(1)}, u32[]{:S(2)}, u32[]{:S(2)}) collective-permute-start(bf16[4,4,144,128]{3,2,1,0:T(8,128)(2,1)S(1)} %gram_mate.1), channel_id=1, source_target_pairs={{0,64},{64,0},{128,192},{192,128},{256,320},{320,256},{384,448},{4... | collective-permute-start | bytes 1769480 | tf_op jit(solution)/shard_map/ppermute | solution.py:342
  15.7 14.4 %copy-start.5 = (f32[3,2,128,128]{3,2,1,0:T(8,128)S(1)}, f32[3,2,128,128]{3,2,1,0:T(8,128)}, u32[]{:S(2)}) copy-start(f32[3,2,128,128]{3,2,1,0:T(8,128)} %steps_ref.1) | copy-start | bytes 1179652
  15.7 14.4 %copy-start.6 = (f32[32]{0:T(128)S(1)}, f32[32]{0:T(128)}, u32[]{:S(2)}) copy-start(f32[32]{0:T(128)} %noise_ref.1) | copy-start | bytes 388
  16.7 13.4 %all-to-all-start = ((bf16[4,4,144,128]{3,2,1,0:T(8,128)(2,1)}), bf16[4,4,144,128]{3,2,1,0:T(8,128)(2,1)S(1)}, u32[]{:S(2)}, u32[]{:S(2)}) async-start(bf16[4,4,144,128]{3,2,1,0:T(8,128)(2,1)} %add_convert_fusion), calls=%async_computation | async-start | bytes 1179648 | tf_op jit(solution)/shard_map/all_to_all | solution.py:332
  20.8 27.7 %copy-start.1 = (bf16[2,32,128,128]{3,2,1,0:T(8,128)(2,1)S(1)}, bf16[2,32,128,128]{3,2,1,0:T(8,128)(2,1)}, u32[]{:S(2)}) copy-start(bf16[2,32,128,128]{3,2,1,0:T(8,128)(2,1)} %chan_ref.7) | copy-start | bytes 6291460
  20.8 27.7 %copy-start.3 = (bf16[2,32,128]{2,1,0:T(8,128)(2,1)S(1)}, bf16[2,32,128]{2,1,0:T(8,128)(2,1)}, u32[]{:S(2)}) copy-start(bf16[2,32,128]{2,1,0:T(8,128)(2,1)} %recv_ref.7) | copy-start | bytes 49156
  45.1 12.7 %all-to-all-start.2 = ((bf16[8,96,128]{2,1,0:T(8,128)(2,1)}), bf16[8,96,128]{2,1,0:T(8,128)(2,1)S(1)}, u32[]{:S(2)}, u32[]{:S(2)}) async-start(bf16[8,96,128]{2,1,0:T(8,128)(2,1)} %broadcast_in_dim.9), calls=%async_computation.2 | async-start | bytes 393216 | tf_op jit(solution)/shard_map/all_to_all | solution.py:332
  58.5 17.1 %all-to-all-start.3 = ((bf16[8,96,128]{2,1,0:T(8,128)(2,1)}), bf16[8,96,128]{2,1,0:T(8,128)(2,1)S(1)}, u32[]{:S(2)}, u32[]{:S(2)}) async-start(bf16[8,96,128]{2,1,0:T(8,128)(2,1)} %broadcast_in_dim.10), calls=%async_computation.3 | async-start | bytes 393216 | tf_op jit(solution)/shard_map/all_to_all | solution.py:332

commit v5 on v4

--- a/solution.py
+++ b/solution.py
@@ -44,58 +44,61 @@
 
 def gram_kernel(own, chan_ref, recv_ref, cot_ref, out_ref, cot_rows):
     panel = lax.axis_index("panel")
-    step = pl.program_id(0)
     core = lax.rem(panel + (0 if own else 1), 2)
 
-    @pl.when(step == 0)
-    def _():
-        place = (iota((16, U), 1) == panel * 16 + iota((16, U), 0)).astype(F32).astype(BF16)
-        for part in range(2):
-            high, low = split(cot_ref[part])
-            cot_rows[2 * part] = dot(high, place, TN)
-            cot_rows[2 * part + 1] = dot(low, place, TN)
-
-    y_rows = jnp.concatenate([recv_ref[0], recv_ref[1]], axis=1)
-    y_rows = jnp.concatenate([y_rows, jnp.zeros_like(y_rows)], axis=0)
+    place = (iota((16, U), 1) == panel * 16 + iota((16, U), 0)).astype(F32).astype(BF16)
+    for part in range(2):
+        high, low = split(cot_ref[part])
+        cot_rows[2 * part] = dot(high, place, TN)
+        cot_rows[2 * part + 1] = dot(low, place, TN)
+
+    received = jnp.concatenate([recv_ref[0].astype(F32), recv_ref[1].astype(F32)], axis=1)
     upper = iota((U, U), 0) <= iota((U, U), 1)
     at = iota((8, 2 * U), 0)
-    for j in range(SUB):
-        row = core * SUB + j
-        h_re, h_im = chan_ref[0, row], chan_ref[1, row]
-        stack = jnp.concatenate([h_re, h_im], axis=0)
-        other = jnp.concatenate([h_im, -h_re], axis=0)
-        both = jnp.concatenate([stack, other], axis=1)
-        left = jnp.concatenate([stack.T, y_rows], axis=0)
-        prod = dot(left, both)
-        packed = jnp.where(upper, prod[:U, :U], prod[:U, U:])
-        match = jnp.sum(jnp.where(at == row, prod[U : U + 8], 0.0), axis=0, keepdims=True)
-        m_re, m_im = match[:, :U], -match[:, U:]
-        m_re_high, m_im_high = m_re.astype(BF16).astype(F32), m_im.astype(BF16).astype(F32)
-        extra = rows_of(
-            [(m_re_high, 0), (m_re - m_re_high, 0), (m_im_high, 0), (m_im - m_im_high, 0)]
-            + [(cot_rows[k, pl.ds(step * 8 + row, 1), :], 0) for k in range(4)],
-            16,
-        )
-        out_ref[0, j, 0:U, :] = packed.astype(BF16)
-        out_ref[0, j, U:ROWS, :] = extra.astype(BF16)
+    for step in range(4):
+        y_rows = received[8 * step : 8 * step + 8]
+        y_rows = jnp.concatenate([y_rows, jnp.zeros_like(y_rows)], axis=0).astype(BF16)
+        for j in range(SUB):
+            row = core * SUB + j
+            h_re, h_im = chan_ref[0, step, 0, j], chan_ref[1, step, 0, j]
+            stack = jnp.concatenate([h_re, h_im], axis=0)
+            other = jnp.concatenate([h_im, -h_re], axis=0)
+            both = jnp.concatenate([stack, other], axis=1)
+            left = jnp.concatenate([stack.T, y_rows], axis=0)
+            prod = dot(left, both)
+            packed = jnp.where(upper, prod[:U, :U], prod[:U, U:])
+            match = jnp.sum(jnp.where(at == row, prod[U : U + 8], 0.0), axis=0, keepdims=True)
+            m_re, m_im = match[:, :U], -match[:, U:]
+            m_re_high, m_im_high = m_re.astype(BF16).astype(F32), m_im.astype(BF16).astype(F32)
+            extra = rows_of(
+                [(m_re_high, 0), (m_re - m_re_high, 0), (m_im_high, 0), (m_im - m_im_high, 0)]
+                + [(cot_rows[k, pl.ds(step * 8 + row, 1), :], 0) for k in range(4)],
+                16,
+            )
+            out_ref[step, j, 0:U, :] = packed.astype(BF16)
+            out_ref[step, j, U:ROWS, :] = extra.astype(BF16)
 
 
 def gram_call(own, channel, received, cot):
+    def place(i):
+        return (0, 0, lax.rem(lax.axis_index("panel") + (0 if own else 1), 2), 0, 0, 0)
+
+    limit = pltpu.CompilerParams(vmem_limit_bytes=8 << 20) if own else pltpu.CompilerParams()
     return pl.pallas_call(
         functools.partial(gram_kernel, own),
-        grid=(4,),
+        grid=(1,),
         out_shape=jax.ShapeDtypeStruct((NP // 2, SUB, ROWS, U), BF16),
         in_specs=[
-            pl.BlockSpec((2, 8, A, U), lambda i: (0, i, 0, 0)),
-            pl.BlockSpec((2, 8, A), lambda i: (0, i, 0)),
+            pl.BlockSpec((2, 4, 1, SUB, A, U), place),
+            pl.BlockSpec((2, 32, A), lambda i: (0, 0, 0)),
             pl.BlockSpec((2, 16, 32), lambda i: (0, 0, 0)),
         ],
-        out_specs=pl.BlockSpec((1, SUB, ROWS, U), lambda i: (i, 0, 0, 0)),
+        out_specs=pl.BlockSpec((NP // 2, SUB, ROWS, U), lambda i: (0, 0, 0, 0)),
         scratch_shapes=[pltpu.VMEM((4, 32, U), F32)],
-        compiler_params=pltpu.CompilerParams(vmem_limit_bytes=8 << 20),
+        compiler_params=limit,
         cost_estimate=pl.CostEstimate(flops=3 * 10**8, bytes_accessed=3 << 20, transcendentals=0),
         name="gram_own" if own else "gram_mate",
-    )(channel, received, cot)
+    )(channel.reshape(2, 4, 2, SUB, A, U), received, cot)
 
 
 def detect_kernel(noise_ref, count_ref, rx_ref, steps_ref, out_ref, gram_w, step_w):

time: 89.1 us -> 87.2 us (0.979)
  local copies, waits for them, and re-layouts: 4.48 us -> 1.46 us
  waiting for transfers between devices: 18.1 us -> 19.3 us
    unnamed x14 -> x10, local copies, waits for them, and re-layouts: 3.05 us -> 0.03 us
    ppermute x1, waiting for transfers between devices: 0.01 us -> 1.17 us  [on_device(): got = lax.ppermute(away, 'panel', [(p, p ^ 1) for p in range(NP)])]
  transfers between devices with their start and end apart: 4 -> 4, of which waited for: 3 -> 4; matrix products, arithmetic and copies ran while one was open for 0% -> 0% of each run, Pallas kernels for 12% -> 11%
where the time goes in v5:
time: 87.2 us; the launch traced here: 86.8 us
  starting transfers between devices  24 us (28%)
  blocking collectives  23.1 us (26%)
  waiting for transfers between devices  19.3 us (22%)
  Pallas kernels  16.5 us (19%)
  local copies, waits for them, and re-layouts  1.46 us (2%)
  between operations  1.4 us (2%)
  other arithmetic  1.06 us (1%)
    all_to_all x2, blocking collectives, exchange(): lax.all_to_all(value, axis, split_axis=0, concat_axis=0, tiled=True, axis...  23.1 us
    all_to_all x3, waiting for transfers between devices, exchange(): lax.all_to_all(value, axis, split_axis=0, concat_axis=0, tiled=True, axis...  18.1 us
    all_to_all x3, starting transfers between devices, exchange(): lax.all_to_all(value, axis, split_axis=0, concat_axis=0, tiled=True, axis...  15.3 us
    pallas_call x2, Pallas kernels, chain_call(): pl.pallas_call(chain_kernel, grid=(2,), out_shape=(jax.ShapeDtypeStruct((...  9.11 us
    ppermute x1, starting transfers between devices, on_device(): got = lax.ppermute(away, 'panel', [(p, p ^ 1) for p in range(NP)])  8.73 us
    pallas_call x2, Pallas kernels, gram_call(): pl.pallas_call(functools.partial(gram_kernel, own), grid=(1,), out_shape=...  3.37 us
    pallas_call x1, Pallas kernels, detect_call(): pl.pallas_call(detect_kernel, out_shape=jax.ShapeDtypeStruct((NP, 160, U)...  3.23 us
  transfers between devices with their start and end apart: 4, of which 4 were waited for; matrix products, arithmetic and copies ran while one was open for 0% of the time, Pallas kernels for 11%

profile of v5, /device:TPU:1, one launch (start us, length us, event | category | flops | bytes accessed | tf_op | source)
XLA Modules:
  0.0 86.8 jit_solution(1842388168335369650)
XLA Ops:
  0.6 0.0 copy-start.1
  0.6 0.0 copy-start
  0.7 0.0 copy-start.2
  0.7 2.8 %gram_mate.1 = bf16[4,4,144,128]{3,2,1,0:T(8,128)(2,1)} custom-call(bf16[2,4,2,4,128,128]{5,4,3,2,1,0:T(8,128)(2,1)} %bitcast.2, bf16[2,32,128]{2,1,0:T(8,128)(2,1)} %recv_ref.7, f32[2,16,32]{2,1,0:T(8,128)} %bitcast.4), custom_call_target="tpu_custom_call" | custom-call | flops 300000000 | bytes 3145728 | tf_op jit(solution)/shard_map/gram_mate/pallas_call | solution.py:87
  3.4 8.7 %collective-permute-start = (bf16[4,4,144,128]{3,2,1,0:T(8,128)(2,1)}, bf16[4,4,144,128]{3,2,1,0:T(8,128)(2,1)S(1)}, u32[]{:S(2)}, u32[]{:S(2)}) collective-permute-start(bf16[4,4,144,128]{3,2,1,0:T(8,128)(2,1)} %gram_mate.1), channel_id=1, source_target_pairs={{0,64},{64,0},{128,192},{192,128},{256,320},{320,256},{384,448},{4... | collective-permute-start | bytes 1769480 | tf_op jit(solution)/shard_map/ppermute | solution.py:345
  12.2 0.0 copy-done.1
  12.2 0.0 copy-done
  12.2 0.0 copy-done.2
  12.2 0.6 gram_own.1
  12.8 0.0 copy-start.3
  12.8 0.0 copy-start.4
  12.8 1.2 %collective-permute-done = bf16[4,4,144,128]{3,2,1,0:T(8,128)(2,1)S(1)} collective-permute-done((bf16[4,4,144,128]{3,2,1,0:T(8,128)(2,1)}, bf16[4,4,144,128]{3,2,1,0:T(8,128)(2,1)S(1)}, u32[]{:S(2)}, u32[]{:S(2)}) %collective-permute-start) | collective-permute-done | bytes 589856 | tf_op jit(solution)/shard_map/ppermute | solution.py:345
  14.0 1.0 %add_convert_fusion = bf16[4,4,144,128]{3,2,1,0:T(8,128)(2,1)} fusion(bf16[4,4,144,128]{3,2,1,0:T(8,128)(2,1)S(1)} %collective-permute-done, bf16[4,4,144,128]{3,2,1,0:T(8,128)(2,1)S(1)} %gram_own.1), kind=kLoop, calls=%fused_computation | loop fusion | flops 1179648 | bytes 1769472 | tf_op jit(solution)/shard_map/convert_element_type | solution.py:347
  15.0 3.5 %all-to-all-start = ((bf16[4,4,144,128]{3,2,1,0:T(8,128)(2,1)}), bf16[4,4,144,128]{3,2,1,0:T(8,128)(2,1)S(1)}, u32[]{:S(2)}, u32[]{:S(2)}) async-start(bf16[4,4,144,128]{3,2,1,0:T(8,128)(2,1)} %add_convert_fusion), calls=%async_computation | async-start | bytes 1179648 | tf_op jit(solution)/shard_map/all_to_all | solution.py:335
  19.1 9.2 %all-to-all-done.rx_ref = bf16[4,4,144,128]{3,2,1,0:T(8,128)(2,1)S(1)} async-done(((bf16[4,4,144,128]{3,2,1,0:T(8,128)(2,1)}), bf16[4,4,144,128]{3,2,1,0:T(8,128)(2,1)S(1)}, u32[]{:S(2)}, u32[]{:S(2)}) %all-to-all-start) | async-done | bytes 589856 | tf_op jit(solution)/shard_map/all_to_all | solution.py:335
  28.3 0.0 copy-done.3
  28.3 0.0 copy-done.4
  28.3 3.2 %detect.1 = bf16[8,160,128]{2,1,0:T(8,128)(2,1)S(1)} custom-call(f32[32]{0:T(128)S(1)} %copy-done.4, s32[1]{0:T(128)S(6)} %copy.13.count_ref, bf16[4,4,144,128]{3,2,1,0:T(8,128)(2,1)S(1)} %all-to-all-done.rx_ref, f32[3,2,128,128]{3,2,1,0:T(8,128)S(1)} %copy-done.3), custom_call_target="tpu_custom_call" | custom-call | flops 1000000000 | bytes 4194304 | tf_op jit(solution)/shard_map/detect/pallas_call | solution.py:243
  31.6 11.1 %all_to_all.25.fac_ref = bf16[8,160,128]{2,1,0:T(8,128)(2,1)S(1)} all-to-all(bf16[8,160,128]{2,1,0:T(8,128)(2,1)S(1)} %detect.1), channel_id=1, replica_groups=mesh['panel'=8,'sc'=64] {'panel'}, dimensions={0} | all-to-all | bytes 655360 | tf_op jit(solution)/shard_map/all_to_all | solution.py:335
  42.7 0.7 broadcast_in_dim.9
  43.4 3.4 %all-to-all-start.2 = ((bf16[8,96,128]{2,1,0:T(8,128)(2,1)}), bf16[8,96,128]{2,1,0:T(8,128)(2,1)S(1)}, u32[]{:S(2)}, u32[]{:S(2)}) async-start(bf16[8,96,128]{2,1,0:T(8,128)(2,1)} %broadcast_in_dim.9), calls=%async_computation.2 | async-start | bytes 393216 | tf_op jit(solution)/shard_map/all_to_all | solution.py:335
  46.8 4.6 %chain_a.1 = (bf16[2,32,128,128]{3,2,1,0:T(8,128)(2,1)}, bf16[2,32,128]{2,1,0:T(8,128)(2,1)}) custom-call(bf16[2,32,128,128]{3,2,1,0:T(8,128)(2,1)S(1)} %copy-done, bf16[2,32,128]{2,1,0:T(8,128)(2,1)S(1)} %copy-done.1, bf16[8,160,128]{2,1,0:T(8,128)(2,1)S(1)} %all_to_all.25.fac_ref), custom_call_target="tpu_custom_call" | custom-call | flops 1000000000 | bytes 12582912 | tf_op jit(solution)/shard_map/chain_a/pallas_call | solution.py:298
  51.3 4.7 %all-to-all-done.2 = bf16[8,96,128]{2,1,0:T(8,128)(2,1)S(1)} async-done(((bf16[8,96,128]{2,1,0:T(8,128)(2,1)}), bf16[8,96,128]{2,1,0:T(8,128)(2,1)S(1)}, u32[]{:S(2)}, u32[]{:S(2)}) %all-to-all-start.2) | async-done | bytes 196640 | tf_op jit(solution)/shard_map/all_to_all | solution.py:335
  56.1 0.7 broadcast_in_dim.10
  56.8 8.4 %all-to-all-start.3 = ((bf16[8,96,128]{2,1,0:T(8,128)(2,1)}), bf16[8,96,128]{2,1,0:T(8,128)(2,1)S(1)}, u32[]{:S(2)}, u32[]{:S(2)}) async-start(bf16[8,96,128]{2,1,0:T(8,128)(2,1)} %broadcast_in_dim.10), calls=%async_computation.3 | async-start | bytes 393216 | tf_op jit(solution)/shard_map/all_to_all | solution.py:335
  65.2 4.6 %chain_b.1 = (bf16[2,32,128,128]{3,2,1,0:T(8,128)(2,1)}, bf16[2,32,128]{2,1,0:T(8,128)(2,1)}) custom-call(bf16[2,32,128,128]{3,2,1,0:T(8,128)(2,1)S(1)} %copy-done, bf16[2,32,128]{2,1,0:T(8,128)(2,1)S(1)} %copy-done.1, bf16[8,160,128]{2,1,0:T(8,128)(2,1)S(1)} %all_to_all.25.fac_ref, ...), custom_call_target="tpu_custom_call", output_to_operand_aliasing={{0}: (3, {}), {1}: (4, {})} | custom-call | flops 1000000000 | bytes 12582912 | tf_op jit(solution)/shard_map/chain_b/pallas_call | solution.py:298
  69.7 4.2 %all-to-all-done.3 = bf16[8,96,128]{2,1,0:T(8,128)(2,1)S(1)} async-done(((bf16[8,96,128]{2,1,0:T(8,128)(2,1)}), bf16[8,96,128]{2,1,0:T(8,128)(2,1)S(1)}, u32[]{:S(2)}, u32[]{:S(2)}) %all-to-all-start.3) | async-done | bytes 196640 | tf_op jit(solution)/shard_map/all_to_all | solution.py:335
  74.0 12.0 %all_to_all.26.in_ref = bf16[8,96,128]{2,1,0:T(8,128)(2,1)S(1)} all-to-all(bf16[8,96,128]{2,1,0:T(8,128)(2,1)S(1)} %broadcast_in_dim.11), channel_id=1, replica_groups=mesh['panel'=8,'sc'=64] {'panel'}, dimensions={0} | all-to-all | bytes 393216 | tf_op jit(solution)/shard_map/all_to_all | solution.py:335
  86.0 0.8 widen.1
  (4 shorter events, 0.1 us)
Async XLA Ops:
  0.6 11.6 %copy-start.1 = (bf16[2,32,128]{2,1,0:T(8,128)(2,1)S(1)}, bf16[2,32,128]{2,1,0:T(8,128)(2,1)}, u32[]{:S(2)}) copy-start(bf16[2,32,128]{2,1,0:T(8,128)(2,1)} %recv_ref.7) | copy-start | bytes 49156
  0.6 11.6 %copy-start = (bf16[2,32,128,128]{3,2,1,0:T(8,128)(2,1)S(1)}, bf16[2,32,128,128]{3,2,1,0:T(8,128)(2,1)}, u32[]{:S(2)}) copy-start(bf16[2,32,128,128]{3,2,1,0:T(8,128)(2,1)} %chan_ref.3) | copy-start | bytes 6291460
  0.7 11.6 %copy-start.2 = (f32[2,32,16]{1,2,0:T(8,128)S(1)}, f32[2,32,16]{1,2,0:T(8,128)}, u32[]{:S(2)}) copy-start(f32[2,32,16]{1,2,0:T(8,128)} %param.10) | copy-start | bytes 12292
  3.4 10.6 %collective-permute-start = (bf16[4,4,144,128]{3,2,1,0:T(8,128)(2,1)}, bf16[4,4,144,128]{3,2,1,0:T(8,128)(2,1)S(1)}, u32[]{:S(2)}, u32[]{:S(2)}) collective-permute-start(bf16[4,4,144,128]{3,2,1,0:T(8,128)(2,1)} %gram_mate.1), channel_id=1, source_target_pairs={{0,64},{64,0},{128,192},{192,128},{256,320},{320,256},{384,448},{4... | collective-permute-start | bytes 1769480 | tf_op jit(solution)/shard_map/ppermute | solution.py:345
  12.8 15.5 %copy-start.3 = (f32[3,2,128,128]{3,2,1,0:T(8,128)S(1)}, f32[3,2,128,128]{3,2,1,0:T(8,128)}, u32[]{:S(2)}) copy-start(f32[3,2,128,128]{3,2,1,0:T(8,128)} %steps_ref.1) | copy-start | bytes 1179652
  12.8 15.5 %copy-start.4 = (f32[32]{0:T(128)S(1)}, f32[32]{0:T(128)}, u32[]{:S(2)}) copy-start(f32[32]{0:T(128)} %noise_ref.1) | copy-start | bytes 388
  15.0 13.4 %all-to-all-start = ((bf16[4,4,144,128]{3,2,1,0:T(8,128)(2,1)}), bf16[4,4,144,128]{3,2,1,0:T(8,128)(2,1)S(1)}, u32[]{:S(2)}, u32[]{:S(2)}) async-start(bf16[4,4,144,128]{3,2,1,0:T(8,128)(2,1)} %add_convert_fusion), calls=%async_computation | async-start | bytes 1179648 | tf_op jit(solution)/shard_map/all_to_all | solution.py:335
  43.4 12.7 %all-to-all-start.2 = ((bf16[8,96,128]{2,1,0:T(8,128)(2,1)}), bf16[8,96,128]{2,1,0:T(8,128)(2,1)S(1)}, u32[]{:S(2)}, u32[]{:S(2)}) async-start(bf16[8,96,128]{2,1,0:T(8,128)(2,1)} %broadcast_in_dim.9), calls=%async_computation.2 | async-start | bytes 393216 | tf_op jit(solution)/shard_map/all_to_all | solution.py:335
  56.8 17.1 %all-to-all-start.3 = ((bf16[8,96,128]{2,1,0:T(8,128)(2,1)}), bf16[8,96,128]{2,1,0:T(8,128)(2,1)S(1)}, u32[]{:S(2)}, u32[]{:S(2)}) async-start(bf16[8,96,128]{2,1,0:T(8,128)(2,1)} %broadcast_in_dim.10), calls=%async_computation.3 | async-start | bytes 393216 | tf_op jit(solution)/shard_map/all_to_all | solution.py:335
